TPU v7x, 512 devices: a whole 4x8x8 slice. The times are simulated.
512 devices in a mesh: tm: 16 (over y_lo, z), chan: 32 (over y_hi, x, core).
Axes of the slice: x: 4, y: 8 (y_hi: 4, y_lo: 2; y = y_hi * 2 + y_lo), z: 8, core: 2. Of those that a mesh axis runs over, the one named last changes fastest.
Arguments:
- raw_strain: bfloat16 [512, 256000], P('chan', 'tm'), may hold values from -80 to 80
Outputs:
- whitened: bfloat16 [128, 512, 512], P(None, 'chan', 'tm')
- cross_spectra: float32 [2, 128, 512, 512], P(None, 'tm', 'chan')
All inputs are finite; a program needn't handle non-finite values.
Results may differ from a plain program's by a relative error of at most 0.0058.
Values may be sent and summed in bfloat16 or wider, within the bound.
A program may use at most 64 MiB of HBM per device.

v0:
```python
import math

import jax
import jax.numpy as jnp
from jax import lax
from jax.sharding import PartitionSpec as P

L = 2000
F = 128
K0 = 8
RM = 250
SMOOTH = 16
HOP = 1000


def from_behind(x, axis, by):
    count = lax.axis_size(axis)
    pairs = [(i, i + by) for i in range(count) if 0 <= i + by < count]
    return lax.ppermute(x, axis, pairs)


def shifted(block, axis, distance):
    devices = range(lax.axis_size(axis))
    route = [((i - distance) % len(devices), i) for i in devices]
    return lax.ppermute(block, axis, route)


def build_table():
    sample_ids = jnp.arange(L, dtype=jnp.int32)[:, None]
    bin_ids = (K0 + jnp.arange(F, dtype=jnp.int32))[None, :]
    turns = (sample_ids * bin_ids % L).astype(jnp.float32) * jnp.float32(2.0 * math.pi / L)
    return jnp.stack([jnp.cos(turns), -jnp.sin(turns)], axis=1).astype(jnp.bfloat16)


def build_kernel():
    positions = jnp.arange(F, dtype=jnp.float32)
    distance = positions[:, None] - positions[None, :]
    weights = jnp.exp(-distance * distance / jnp.float32(2.0 * SMOOTH * SMOOTH))
    return weights / jnp.sum(weights, axis=1, keepdims=True)


def prefix_sums(values):
    rows, length = values.shape
    block_len = 256
    blocks = (length + block_len - 1) // block_len
    padded = jnp.pad(values, ((0, 0), (0, blocks * block_len - length)))
    shaped = padded.reshape(rows, blocks, block_len)
    inner = jnp.cumsum(shaped, axis=2)
    totals = inner[:, :, block_len - 1]
    offsets = jnp.cumsum(totals, axis=1) - totals
    running = (inner + offsets[:, :, None]).reshape(rows, blocks * block_len)[:, :length]
    return jnp.concatenate([jnp.zeros((rows, 1), jnp.float32), running], axis=1)


def normalize(extended):
    box_width = 2 * RM + 1
    length = extended.shape[1]
    count = length - 2 * RM
    running = prefix_sums(jnp.abs(extended))
    box_sums = running[:, box_width : box_width + count] - running[:, :count]
    abs_level = box_sums / box_width
    inner = extended[:, RM : length - RM]
    return (inner / (abs_level + 1e-06)).astype(jnp.bfloat16)


def on_device(raw_strain):
    per_group, samples = raw_strain.shape
    windows = samples // HOP
    lead_rim = from_behind(raw_strain[:, samples - RM :], "tm", 1)
    tail_rim = from_behind(raw_strain[:, : HOP + RM], "tm", -1)
    extended = jnp.concatenate([lead_rim, raw_strain, tail_rim], axis=1).astype(jnp.float32)
    normalized = normalize(extended)
    pieces = normalized.reshape(per_group, windows + 1, HOP)
    frames = jnp.concatenate([pieces[:, :-1], pieces[:, 1:]], axis=2)
    spectrum = jnp.einsum(
        "cwl,lrf->fcrw", frames, build_table(), preferred_element_type=jnp.float32
    )
    energy = spectrum[:, :, 0] * spectrum[:, :, 0] + spectrum[:, :, 1] * spectrum[:, :, 1]
    smoothed = jnp.einsum("gf,fcw->gcw", build_kernel(), energy, precision=lax.Precision.HIGHEST)
    whitened = (spectrum * lax.rsqrt(smoothed + 1e-06)[:, :, None]).astype(jnp.bfloat16)
    stored = whitened.reshape(F, per_group, 2 * windows)
    owned = lax.all_to_all(stored, "tm", split_axis=0, concat_axis=2, tiled=True)
    own_bins, _, lane_depth = owned.shape
    window_total = lane_depth // 2
    time_count = lax.axis_size("tm")
    split_parts = owned.reshape(own_bins, per_group, time_count, 2, windows)
    flipped = jnp.stack([split_parts[:, :, :, 1], -split_parts[:, :, :, 0]], axis=3).reshape(
        own_bins, per_group, lane_depth
    )
    left_side = jnp.concatenate([owned, flipped], axis=1)

    def pair_block(visiting):
        product = lax.dot_general(
            left_side, visiting, (((2,), (2,)), ((0,), (0,))), preferred_element_type=jnp.float32
        )
        return (
            jnp.transpose(product.reshape(own_bins, 2, per_group, per_group), (1, 0, 2, 3))
            / window_total
        )

    chan_count = lax.axis_size("chan")
    my_group = lax.axis_index("chan")
    anchor = jnp.int32(0)

    def insert_block(stacked_sum, result_block, source_group):
        return lax.dynamic_update_slice(
            stacked_sum, result_block, (anchor, anchor, anchor, source_group * per_group)
        )

    stacked_sum = jnp.zeros((2, own_bins, per_group, per_group * chan_count), jnp.float32)
    stacked_sum = insert_block(stacked_sum, pair_block(owned), my_group)

    def advance(turn_index, state_pair):
        visiting, running = state_pair
        visiting = shifted(visiting, "chan", 1)
        source_group = (my_group - turn_index) % chan_count
        return (visiting, insert_block(running, pair_block(visiting), source_group))

    _, stacked_sum = lax.fori_loop(1, chan_count, advance, (owned, stacked_sum))
    return (stored, stacked_sum)


def solution(mesh):
    placed = (P("chan", "tm"),)
    return jax.shard_map(
        on_device,
        mesh=mesh,
        in_specs=placed,
        out_specs=(P(None, "chan", "tm"), P(None, "tm", "chan", None)),
        check_vma=False,
    )
```

profile of v0, /device:TPU:8, one launch (start us, length us, event | category | flops | bytes accessed | tf_op | source)
XLA Modules:
  0.0 444.1 jit_solution(137696240015219215)
XLA Ops:
  22.7 9.6 %reduce-window.6 = f32[16,69,2,128]{3,1,2,0:T(8,128)S(1)} reduce-window(f32[16,69,2,128]{3,1,2,0:T(8,128)S(1)} %copy.19, f32[]{:T(128)} %constant.114.clone.1), window={size=1x1x1x128 pad=0_0x0_0x0_0x127_0}, to_apply=%region_0.1 | reduce-window | flops 35893248 | bytes 2260996 | tf_op jit(solution)/shard_map/reduce-window
  71.1 366.7 %while.17 = (s32[]{:T(128)}, bf16[8,16,512]{2,1,0:T(8,128)(2,1)S(1)}, f32[2,8,16,512]{2,0,3,1:T(2,128)}, bf16[8,32,512]{2,1,0:T(8,128)(2,1)S(1)}, s32[]{:T(128)}...) while((s32[]{:T(128)}, bf16[8,16,512]{2,1,0:T(8,128)(2,1)S(1)}, ...), condition=%wide.region_5.6_spmd, body=%wide.region_4.5_spmd.sunk | while | flops 4198418 | bytes 1376576 | solution.py:119
  73.0 9.6 %collective-permute-done = bf16[8,16,512]{2,1,0:T(8,128)(2,1)S(1)} collective-permute-done((bf16[8,16,512]{2,1,0:T(8,128)(2,1)S(1)}, bf16[8,16,512]{2,1,0:T(8,128)(2,1)S(1)}, u32[]{:S(2)}, u32[]{:S(2)}) %collective-permute-start) | collective-permute-done | bytes 131104 | tf_op jit(solution)/shard_map/while/body/eval_jaxpr/ppermute | solution.py:25
  85.6 9.7 %collective-permute-done = bf16[8,16,512]{2,1,0:T(8,128)(2,1)S(1)} collective-permute-done((bf16[8,16,512]{2,1,0:T(8,128)(2,1)S(1)}, bf16[8,16,512]{2,1,0:T(8,128)(2,1)S(1)}, u32[]{:S(2)}, u32[]{:S(2)}) %collective-permute-start) | collective-permute-done | bytes 131104 | tf_op jit(solution)/shard_map/while/body/eval_jaxpr/ppermute | solution.py:25
  98.3 10.0 %collective-permute-done = bf16[8,16,512]{2,1,0:T(8,128)(2,1)S(1)} collective-permute-done((bf16[8,16,512]{2,1,0:T(8,128)(2,1)S(1)}, bf16[8,16,512]{2,1,0:T(8,128)(2,1)S(1)}, u32[]{:S(2)}, u32[]{:S(2)}) %collective-permute-start) | collective-permute-done | bytes 131104 | tf_op jit(solution)/shard_map/while/body/eval_jaxpr/ppermute | solution.py:25
  111.3 9.6 %collective-permute-done = bf16[8,16,512]{2,1,0:T(8,128)(2,1)S(1)} collective-permute-done((bf16[8,16,512]{2,1,0:T(8,128)(2,1)S(1)}, bf16[8,16,512]{2,1,0:T(8,128)(2,1)S(1)}, u32[]{:S(2)}, u32[]{:S(2)}) %collective-permute-start) | collective-permute-done | bytes 131104 | tf_op jit(solution)/shard_map/while/body/eval_jaxpr/ppermute | solution.py:25
  123.9 8.7 %collective-permute-done = bf16[8,16,512]{2,1,0:T(8,128)(2,1)S(1)} collective-permute-done((bf16[8,16,512]{2,1,0:T(8,128)(2,1)S(1)}, bf16[8,16,512]{2,1,0:T(8,128)(2,1)S(1)}, u32[]{:S(2)}, u32[]{:S(2)}) %collective-permute-start) | collective-permute-done | bytes 131104 | tf_op jit(solution)/shard_map/while/body/eval_jaxpr/ppermute | solution.py:25
  135.6 8.6 %collective-permute-done = bf16[8,16,512]{2,1,0:T(8,128)(2,1)S(1)} collective-permute-done((bf16[8,16,512]{2,1,0:T(8,128)(2,1)S(1)}, bf16[8,16,512]{2,1,0:T(8,128)(2,1)S(1)}, u32[]{:S(2)}, u32[]{:S(2)}) %collective-permute-start) | collective-permute-done | bytes 131104 | tf_op jit(solution)/shard_map/while/body/eval_jaxpr/ppermute | solution.py:25
  147.1 8.7 %collective-permute-done = bf16[8,16,512]{2,1,0:T(8,128)(2,1)S(1)} collective-permute-done((bf16[8,16,512]{2,1,0:T(8,128)(2,1)S(1)}, bf16[8,16,512]{2,1,0:T(8,128)(2,1)S(1)}, u32[]{:S(2)}, u32[]{:S(2)}) %collective-permute-start) | collective-permute-done | bytes 131104 | tf_op jit(solution)/shard_map/while/body/eval_jaxpr/ppermute | solution.py:25
  158.9 8.7 %collective-permute-done = bf16[8,16,512]{2,1,0:T(8,128)(2,1)S(1)} collective-permute-done((bf16[8,16,512]{2,1,0:T(8,128)(2,1)S(1)}, bf16[8,16,512]{2,1,0:T(8,128)(2,1)S(1)}, u32[]{:S(2)}, u32[]{:S(2)}) %collective-permute-start) | collective-permute-done | bytes 131104 | tf_op jit(solution)/shard_map/while/body/eval_jaxpr/ppermute | solution.py:25
  170.6 8.7 %collective-permute-done = bf16[8,16,512]{2,1,0:T(8,128)(2,1)S(1)} collective-permute-done((bf16[8,16,512]{2,1,0:T(8,128)(2,1)S(1)}, bf16[8,16,512]{2,1,0:T(8,128)(2,1)S(1)}, u32[]{:S(2)}, u32[]{:S(2)}) %collective-permute-start) | collective-permute-done | bytes 131104 | tf_op jit(solution)/shard_map/while/body/eval_jaxpr/ppermute | solution.py:25
  182.2 8.7 %collective-permute-done = bf16[8,16,512]{2,1,0:T(8,128)(2,1)S(1)} collective-permute-done((bf16[8,16,512]{2,1,0:T(8,128)(2,1)S(1)}, bf16[8,16,512]{2,1,0:T(8,128)(2,1)S(1)}, u32[]{:S(2)}, u32[]{:S(2)}) %collective-permute-start) | collective-permute-done | bytes 131104 | tf_op jit(solution)/shard_map/while/body/eval_jaxpr/ppermute | solution.py:25
  193.9 8.7 %collective-permute-done = bf16[8,16,512]{2,1,0:T(8,128)(2,1)S(1)} collective-permute-done((bf16[8,16,512]{2,1,0:T(8,128)(2,1)S(1)}, bf16[8,16,512]{2,1,0:T(8,128)(2,1)S(1)}, u32[]{:S(2)}, u32[]{:S(2)}) %collective-permute-start) | collective-permute-done | bytes 131104 | tf_op jit(solution)/shard_map/while/body/eval_jaxpr/ppermute | solution.py:25
  205.6 8.7 %collective-permute-done = bf16[8,16,512]{2,1,0:T(8,128)(2,1)S(1)} collective-permute-done((bf16[8,16,512]{2,1,0:T(8,128)(2,1)S(1)}, bf16[8,16,512]{2,1,0:T(8,128)(2,1)S(1)}, u32[]{:S(2)}, u32[]{:S(2)}) %collective-permute-start) | collective-permute-done | bytes 131104 | tf_op jit(solution)/shard_map/while/body/eval_jaxpr/ppermute | solution.py:25
  217.2 8.7 %collective-permute-done = bf16[8,16,512]{2,1,0:T(8,128)(2,1)S(1)} collective-permute-done((bf16[8,16,512]{2,1,0:T(8,128)(2,1)S(1)}, bf16[8,16,512]{2,1,0:T(8,128)(2,1)S(1)}, u32[]{:S(2)}, u32[]{:S(2)}) %collective-permute-start) | collective-permute-done | bytes 131104 | tf_op jit(solution)/shard_map/while/body/eval_jaxpr/ppermute | solution.py:25
  228.9 8.7 %collective-permute-done = bf16[8,16,512]{2,1,0:T(8,128)(2,1)S(1)} collective-permute-done((bf16[8,16,512]{2,1,0:T(8,128)(2,1)S(1)}, bf16[8,16,512]{2,1,0:T(8,128)(2,1)S(1)}, u32[]{:S(2)}, u32[]{:S(2)}) %collective-permute-start) | collective-permute-done | bytes 131104 | tf_op jit(solution)/shard_map/while/body/eval_jaxpr/ppermute | solution.py:25
  240.6 9.4 %collective-permute-done = bf16[8,16,512]{2,1,0:T(8,128)(2,1)S(1)} collective-permute-done((bf16[8,16,512]{2,1,0:T(8,128)(2,1)S(1)}, bf16[8,16,512]{2,1,0:T(8,128)(2,1)S(1)}, u32[]{:S(2)}, u32[]{:S(2)}) %collective-permute-start) | collective-permute-done | bytes 131104 | tf_op jit(solution)/shard_map/while/body/eval_jaxpr/ppermute | solution.py:25
  253.0 8.7 %collective-permute-done = bf16[8,16,512]{2,1,0:T(8,128)(2,1)S(1)} collective-permute-done((bf16[8,16,512]{2,1,0:T(8,128)(2,1)S(1)}, bf16[8,16,512]{2,1,0:T(8,128)(2,1)S(1)}, u32[]{:S(2)}, u32[]{:S(2)}) %collective-permute-start) | collective-permute-done | bytes 131104 | tf_op jit(solution)/shard_map/while/body/eval_jaxpr/ppermute | solution.py:25
  264.7 8.7 %collective-permute-done = bf16[8,16,512]{2,1,0:T(8,128)(2,1)S(1)} collective-permute-done((bf16[8,16,512]{2,1,0:T(8,128)(2,1)S(1)}, bf16[8,16,512]{2,1,0:T(8,128)(2,1)S(1)}, u32[]{:S(2)}, u32[]{:S(2)}) %collective-permute-start) | collective-permute-done | bytes 131104 | tf_op jit(solution)/shard_map/while/body/eval_jaxpr/ppermute | solution.py:25
  276.4 8.7 %collective-permute-done = bf16[8,16,512]{2,1,0:T(8,128)(2,1)S(1)} collective-permute-done((bf16[8,16,512]{2,1,0:T(8,128)(2,1)S(1)}, bf16[8,16,512]{2,1,0:T(8,128)(2,1)S(1)}, u32[]{:S(2)}, u32[]{:S(2)}) %collective-permute-start) | collective-permute-done | bytes 131104 | tf_op jit(solution)/shard_map/while/body/eval_jaxpr/ppermute | solution.py:25
  288.1 8.7 %collective-permute-done = bf16[8,16,512]{2,1,0:T(8,128)(2,1)S(1)} collective-permute-done((bf16[8,16,512]{2,1,0:T(8,128)(2,1)S(1)}, bf16[8,16,512]{2,1,0:T(8,128)(2,1)S(1)}, u32[]{:S(2)}, u32[]{:S(2)}) %collective-permute-start) | collective-permute-done | bytes 131104 | tf_op jit(solution)/shard_map/while/body/eval_jaxpr/ppermute | solution.py:25
  299.8 8.7 %collective-permute-done = bf16[8,16,512]{2,1,0:T(8,128)(2,1)S(1)} collective-permute-done((bf16[8,16,512]{2,1,0:T(8,128)(2,1)S(1)}, bf16[8,16,512]{2,1,0:T(8,128)(2,1)S(1)}, u32[]{:S(2)}, u32[]{:S(2)}) %collective-permute-start) | collective-permute-done | bytes 131104 | tf_op jit(solution)/shard_map/while/body/eval_jaxpr/ppermute | solution.py:25
  311.4 8.7 %collective-permute-done = bf16[8,16,512]{2,1,0:T(8,128)(2,1)S(1)} collective-permute-done((bf16[8,16,512]{2,1,0:T(8,128)(2,1)S(1)}, bf16[8,16,512]{2,1,0:T(8,128)(2,1)S(1)}, u32[]{:S(2)}, u32[]{:S(2)}) %collective-permute-start) | collective-permute-done | bytes 131104 | tf_op jit(solution)/shard_map/while/body/eval_jaxpr/ppermute | solution.py:25
  323.1 8.7 %collective-permute-done = bf16[8,16,512]{2,1,0:T(8,128)(2,1)S(1)} collective-permute-done((bf16[8,16,512]{2,1,0:T(8,128)(2,1)S(1)}, bf16[8,16,512]{2,1,0:T(8,128)(2,1)S(1)}, u32[]{:S(2)}, u32[]{:S(2)}) %collective-permute-start) | collective-permute-done | bytes 131104 | tf_op jit(solution)/shard_map/while/body/eval_jaxpr/ppermute | solution.py:25
  334.8 8.7 %collective-permute-done = bf16[8,16,512]{2,1,0:T(8,128)(2,1)S(1)} collective-permute-done((bf16[8,16,512]{2,1,0:T(8,128)(2,1)S(1)}, bf16[8,16,512]{2,1,0:T(8,128)(2,1)S(1)}, u32[]{:S(2)}, u32[]{:S(2)}) %collective-permute-start) | collective-permute-done | bytes 131104 | tf_op jit(solution)/shard_map/while/body/eval_jaxpr/ppermute | solution.py:25
  346.5 8.7 %collective-permute-done = bf16[8,16,512]{2,1,0:T(8,128)(2,1)S(1)} collective-permute-done((bf16[8,16,512]{2,1,0:T(8,128)(2,1)S(1)}, bf16[8,16,512]{2,1,0:T(8,128)(2,1)S(1)}, u32[]{:S(2)}, u32[]{:S(2)}) %collective-permute-start) | collective-permute-done | bytes 131104 | tf_op jit(solution)/shard_map/while/body/eval_jaxpr/ppermute | solution.py:25
  358.2 8.7 %collective-permute-done = bf16[8,16,512]{2,1,0:T(8,128)(2,1)S(1)} collective-permute-done((bf16[8,16,512]{2,1,0:T(8,128)(2,1)S(1)}, bf16[8,16,512]{2,1,0:T(8,128)(2,1)S(1)}, u32[]{:S(2)}, u32[]{:S(2)}) %collective-permute-start) | collective-permute-done | bytes 131104 | tf_op jit(solution)/shard_map/while/body/eval_jaxpr/ppermute | solution.py:25
  369.9 8.7 %collective-permute-done = bf16[8,16,512]{2,1,0:T(8,128)(2,1)S(1)} collective-permute-done((bf16[8,16,512]{2,1,0:T(8,128)(2,1)S(1)}, bf16[8,16,512]{2,1,0:T(8,128)(2,1)S(1)}, u32[]{:S(2)}, u32[]{:S(2)}) %collective-permute-start) | collective-permute-done | bytes 131104 | tf_op jit(solution)/shard_map/while/body/eval_jaxpr/ppermute | solution.py:25
  381.5 8.7 %collective-permute-done = bf16[8,16,512]{2,1,0:T(8,128)(2,1)S(1)} collective-permute-done((bf16[8,16,512]{2,1,0:T(8,128)(2,1)S(1)}, bf16[8,16,512]{2,1,0:T(8,128)(2,1)S(1)}, u32[]{:S(2)}, u32[]{:S(2)}) %collective-permute-start) | collective-permute-done | bytes 131104 | tf_op jit(solution)/shard_map/while/body/eval_jaxpr/ppermute | solution.py:25
  393.2 8.7 %collective-permute-done = bf16[8,16,512]{2,1,0:T(8,128)(2,1)S(1)} collective-permute-done((bf16[8,16,512]{2,1,0:T(8,128)(2,1)S(1)}, bf16[8,16,512]{2,1,0:T(8,128)(2,1)S(1)}, u32[]{:S(2)}, u32[]{:S(2)}) %collective-permute-start) | collective-permute-done | bytes 131104 | tf_op jit(solution)/shard_map/while/body/eval_jaxpr/ppermute | solution.py:25
  404.9 8.7 %collective-permute-done = bf16[8,16,512]{2,1,0:T(8,128)(2,1)S(1)} collective-permute-done((bf16[8,16,512]{2,1,0:T(8,128)(2,1)S(1)}, bf16[8,16,512]{2,1,0:T(8,128)(2,1)S(1)}, u32[]{:S(2)}, u32[]{:S(2)}) %collective-permute-start) | collective-permute-done | bytes 131104 | tf_op jit(solution)/shard_map/while/body/eval_jaxpr/ppermute | solution.py:25
  416.6 8.7 %collective-permute-done = bf16[8,16,512]{2,1,0:T(8,128)(2,1)S(1)} collective-permute-done((bf16[8,16,512]{2,1,0:T(8,128)(2,1)S(1)}, bf16[8,16,512]{2,1,0:T(8,128)(2,1)S(1)}, u32[]{:S(2)}, u32[]{:S(2)}) %collective-permute-start) | collective-permute-done | bytes 131104 | tf_op jit(solution)/shard_map/while/body/eval_jaxpr/ppermute | solution.py:25
  (227 shorter events, 167.3 us)
Async XLA Ops:
  1.5 18.7 %collective-permute-start.1 = (bf16[16,250]{1,0:T(8,128)(2,1)S(1)}, bf16[16,250]{1,0:T(8,128)(2,1)S(1)}, u32[]{:S(2)}, u32[]{:S(2)}) collective-permute-start(bf16[16,250]{1,0:T(8,128)(2,1)S(1)} %slice.48), channel_id=1, source_target_pairs={{0,32},{32,64},{64,96},{96,128},{128,160},{160,192},{192,224},{224... | collective-permute-start | bytes 24008 | tf_op jit(solution)/shard_map/ppermute | solution.py:19
  6.5 13.7 %collective-permute-start.2 = (bf16[16,1250]{1,0:T(8,128)(2,1)S(1)}, bf16[16,1250]{1,0:T(8,128)(2,1)S(1)}, u32[]{:S(2)}, u32[]{:S(2)}) collective-permute-start(bf16[16,1250]{1,0:T(8,128)(2,1)S(1)} %slice.49), channel_id=1, source_target_pairs={{32,0},{64,32},{96,64},{128,96},{160,128},{192,160},{224,192},{256... | collective-permute-start | bytes 120008 | tf_op jit(solution)/shard_map/ppermute | solution.py:19
  45.1 13.4 %all-to-all-start = ((bf16[16,2,2048]{2,1,0:T(2,128)(2,1)}), bf16[16,2,2048]{2,1,0:T(2,128)(2,1)S(1)}, u32[]{:S(2)}, u32[]{:S(2)}) async-start(bf16[16,2,2048]{2,1,0:T(2,128)(2,1)} %reshape.150), calls=%async_computation | async-start | bytes 262144 | tf_op jit(solution)/shard_map/all_to_all | solution.py:82
  71.1 11.5 %collective-permute-start = (bf16[8,16,512]{2,1,0:T(8,128)(2,1)S(1)}, bf16[8,16,512]{2,1,0:T(8,128)(2,1)S(1)}, u32[]{:S(2)}, u32[]{:S(2)}) collective-permute-start(bf16[8,16,512]{2,1,0:T(8,128)(2,1)S(1)} %get-tuple-element.201), channel_id=1, source_target_pairs={{31,0},{0,1},{1,2},{2,3},{3,4},{4,5},{5,6},{6,7},{7,8},{8,9},{9,10... | collective-permute-start | bytes 393224 | tf_op jit(solution)/shard_map/while/body/eval_jaxpr/ppermute | solution.py:25
  83.7 11.6 %collective-permute-start = (bf16[8,16,512]{2,1,0:T(8,128)(2,1)S(1)}, bf16[8,16,512]{2,1,0:T(8,128)(2,1)S(1)}, u32[]{:S(2)}, u32[]{:S(2)}) collective-permute-start(bf16[8,16,512]{2,1,0:T(8,128)(2,1)S(1)} %get-tuple-element.201), channel_id=1, source_target_pairs={{31,0},{0,1},{1,2},{2,3},{3,4},{4,5},{5,6},{6,7},{7,8},{8,9},{9,10... | collective-permute-start | bytes 393224 | tf_op jit(solution)/shard_map/while/body/eval_jaxpr/ppermute | solution.py:25
  96.3 11.9 %collective-permute-start = (bf16[8,16,512]{2,1,0:T(8,128)(2,1)S(1)}, bf16[8,16,512]{2,1,0:T(8,128)(2,1)S(1)}, u32[]{:S(2)}, u32[]{:S(2)}) collective-permute-start(bf16[8,16,512]{2,1,0:T(8,128)(2,1)S(1)} %get-tuple-element.201), channel_id=1, source_target_pairs={{31,0},{0,1},{1,2},{2,3},{3,4},{4,5},{5,6},{6,7},{7,8},{8,9},{9,10... | collective-permute-start | bytes 393224 | tf_op jit(solution)/shard_map/while/body/eval_jaxpr/ppermute | solution.py:25
  109.3 11.6 %collective-permute-start = (bf16[8,16,512]{2,1,0:T(8,128)(2,1)S(1)}, bf16[8,16,512]{2,1,0:T(8,128)(2,1)S(1)}, u32[]{:S(2)}, u32[]{:S(2)}) collective-permute-start(bf16[8,16,512]{2,1,0:T(8,128)(2,1)S(1)} %get-tuple-element.201), channel_id=1, source_target_pairs={{31,0},{0,1},{1,2},{2,3},{3,4},{4,5},{5,6},{6,7},{7,8},{8,9},{9,10... | collective-permute-start | bytes 393224 | tf_op jit(solution)/shard_map/while/body/eval_jaxpr/ppermute | solution.py:25
  121.9 10.6 %collective-permute-start = (bf16[8,16,512]{2,1,0:T(8,128)(2,1)S(1)}, bf16[8,16,512]{2,1,0:T(8,128)(2,1)S(1)}, u32[]{:S(2)}, u32[]{:S(2)}) collective-permute-start(bf16[8,16,512]{2,1,0:T(8,128)(2,1)S(1)} %get-tuple-element.201), channel_id=1, source_target_pairs={{31,0},{0,1},{1,2},{2,3},{3,4},{4,5},{5,6},{6,7},{7,8},{8,9},{9,10... | collective-permute-start | bytes 393224 | tf_op jit(solution)/shard_map/while/body/eval_jaxpr/ppermute | solution.py:25
  145.2 10.6 %collective-permute-start = (bf16[8,16,512]{2,1,0:T(8,128)(2,1)S(1)}, bf16[8,16,512]{2,1,0:T(8,128)(2,1)S(1)}, u32[]{:S(2)}, u32[]{:S(2)}) collective-permute-start(bf16[8,16,512]{2,1,0:T(8,128)(2,1)S(1)} %get-tuple-element.201), channel_id=1, source_target_pairs={{31,0},{0,1},{1,2},{2,3},{3,4},{4,5},{5,6},{6,7},{7,8},{8,9},{9,10... | collective-permute-start | bytes 393224 | tf_op jit(solution)/shard_map/while/body/eval_jaxpr/ppermute | solution.py:25
  156.9 10.6 %collective-permute-start = (bf16[8,16,512]{2,1,0:T(8,128)(2,1)S(1)}, bf16[8,16,512]{2,1,0:T(8,128)(2,1)S(1)}, u32[]{:S(2)}, u32[]{:S(2)}) collective-permute-start(bf16[8,16,512]{2,1,0:T(8,128)(2,1)S(1)} %get-tuple-element.201), channel_id=1, source_target_pairs={{31,0},{0,1},{1,2},{2,3},{3,4},{4,5},{5,6},{6,7},{7,8},{8,9},{9,10... | collective-permute-start | bytes 393224 | tf_op jit(solution)/shard_map/while/body/eval_jaxpr/ppermute | solution.py:25
  168.6 10.6 %collective-permute-start = (bf16[8,16,512]{2,1,0:T(8,128)(2,1)S(1)}, bf16[8,16,512]{2,1,0:T(8,128)(2,1)S(1)}, u32[]{:S(2)}, u32[]{:S(2)}) collective-permute-start(bf16[8,16,512]{2,1,0:T(8,128)(2,1)S(1)} %get-tuple-element.201), channel_id=1, source_target_pairs={{31,0},{0,1},{1,2},{2,3},{3,4},{4,5},{5,6},{6,7},{7,8},{8,9},{9,10... | collective-permute-start | bytes 393224 | tf_op jit(solution)/shard_map/while/body/eval_jaxpr/ppermute | solution.py:25
  180.3 10.6 %collective-permute-start = (bf16[8,16,512]{2,1,0:T(8,128)(2,1)S(1)}, bf16[8,16,512]{2,1,0:T(8,128)(2,1)S(1)}, u32[]{:S(2)}, u32[]{:S(2)}) collective-permute-start(bf16[8,16,512]{2,1,0:T(8,128)(2,1)S(1)} %get-tuple-element.201), channel_id=1, source_target_pairs={{31,0},{0,1},{1,2},{2,3},{3,4},{4,5},{5,6},{6,7},{7,8},{8,9},{9,10... | collective-permute-start | bytes 393224 | tf_op jit(solution)/shard_map/while/body/eval_jaxpr/ppermute | solution.py:25
  192.0 10.6 %collective-permute-start = (bf16[8,16,512]{2,1,0:T(8,128)(2,1)S(1)}, bf16[8,16,512]{2,1,0:T(8,128)(2,1)S(1)}, u32[]{:S(2)}, u32[]{:S(2)}) collective-permute-start(bf16[8,16,512]{2,1,0:T(8,128)(2,1)S(1)} %get-tuple-element.201), channel_id=1, source_target_pairs={{31,0},{0,1},{1,2},{2,3},{3,4},{4,5},{5,6},{6,7},{7,8},{8,9},{9,10... | collective-permute-start | bytes 393224 | tf_op jit(solution)/shard_map/while/body/eval_jaxpr/ppermute | solution.py:25
  203.6 10.6 %collective-permute-start = (bf16[8,16,512]{2,1,0:T(8,128)(2,1)S(1)}, bf16[8,16,512]{2,1,0:T(8,128)(2,1)S(1)}, u32[]{:S(2)}, u32[]{:S(2)}) collective-permute-start(bf16[8,16,512]{2,1,0:T(8,128)(2,1)S(1)} %get-tuple-element.201), channel_id=1, source_target_pairs={{31,0},{0,1},{1,2},{2,3},{3,4},{4,5},{5,6},{6,7},{7,8},{8,9},{9,10... | collective-permute-start | bytes 393224 | tf_op jit(solution)/shard_map/while/body/eval_jaxpr/ppermute | solution.py:25
  215.3 10.6 %collective-permute-start = (bf16[8,16,512]{2,1,0:T(8,128)(2,1)S(1)}, bf16[8,16,512]{2,1,0:T(8,128)(2,1)S(1)}, u32[]{:S(2)}, u32[]{:S(2)}) collective-permute-start(bf16[8,16,512]{2,1,0:T(8,128)(2,1)S(1)} %get-tuple-element.201), channel_id=1, source_target_pairs={{31,0},{0,1},{1,2},{2,3},{3,4},{4,5},{5,6},{6,7},{7,8},{8,9},{9,10... | collective-permute-start | bytes 393224 | tf_op jit(solution)/shard_map/while/body/eval_jaxpr/ppermute | solution.py:25
  227.0 10.6 %collective-permute-start = (bf16[8,16,512]{2,1,0:T(8,128)(2,1)S(1)}, bf16[8,16,512]{2,1,0:T(8,128)(2,1)S(1)}, u32[]{:S(2)}, u32[]{:S(2)}) collective-permute-start(bf16[8,16,512]{2,1,0:T(8,128)(2,1)S(1)} %get-tuple-element.201), channel_id=1, source_target_pairs={{31,0},{0,1},{1,2},{2,3},{3,4},{4,5},{5,6},{6,7},{7,8},{8,9},{9,10... | collective-permute-start | bytes 393224 | tf_op jit(solution)/shard_map/while/body/eval_jaxpr/ppermute | solution.py:25
  238.6 11.3 %collective-permute-start = (bf16[8,16,512]{2,1,0:T(8,128)(2,1)S(1)}, bf16[8,16,512]{2,1,0:T(8,128)(2,1)S(1)}, u32[]{:S(2)}, u32[]{:S(2)}) collective-permute-start(bf16[8,16,512]{2,1,0:T(8,128)(2,1)S(1)} %get-tuple-element.201), channel_id=1, source_target_pairs={{31,0},{0,1},{1,2},{2,3},{3,4},{4,5},{5,6},{6,7},{7,8},{8,9},{9,10... | collective-permute-start | bytes 393224 | tf_op jit(solution)/shard_map/while/body/eval_jaxpr/ppermute | solution.py:25
  251.0 10.6 %collective-permute-start = (bf16[8,16,512]{2,1,0:T(8,128)(2,1)S(1)}, bf16[8,16,512]{2,1,0:T(8,128)(2,1)S(1)}, u32[]{:S(2)}, u32[]{:S(2)}) collective-permute-start(bf16[8,16,512]{2,1,0:T(8,128)(2,1)S(1)} %get-tuple-element.201), channel_id=1, source_target_pairs={{31,0},{0,1},{1,2},{2,3},{3,4},{4,5},{5,6},{6,7},{7,8},{8,9},{9,10... | collective-permute-start | bytes 393224 | tf_op jit(solution)/shard_map/while/body/eval_jaxpr/ppermute | solution.py:25
  262.7 10.6 %collective-permute-start = (bf16[8,16,512]{2,1,0:T(8,128)(2,1)S(1)}, bf16[8,16,512]{2,1,0:T(8,128)(2,1)S(1)}, u32[]{:S(2)}, u32[]{:S(2)}) collective-permute-start(bf16[8,16,512]{2,1,0:T(8,128)(2,1)S(1)} %get-tuple-element.201), channel_id=1, source_target_pairs={{31,0},{0,1},{1,2},{2,3},{3,4},{4,5},{5,6},{6,7},{7,8},{8,9},{9,10... | collective-permute-start | bytes 393224 | tf_op jit(solution)/shard_map/while/body/eval_jaxpr/ppermute | solution.py:25
  274.4 10.6 %collective-permute-start = (bf16[8,16,512]{2,1,0:T(8,128)(2,1)S(1)}, bf16[8,16,512]{2,1,0:T(8,128)(2,1)S(1)}, u32[]{:S(2)}, u32[]{:S(2)}) collective-permute-start(bf16[8,16,512]{2,1,0:T(8,128)(2,1)S(1)} %get-tuple-element.201), channel_id=1, source_target_pairs={{31,0},{0,1},{1,2},{2,3},{3,4},{4,5},{5,6},{6,7},{7,8},{8,9},{9,10... | collective-permute-start | bytes 393224 | tf_op jit(solution)/shard_map/while/body/eval_jaxpr/ppermute | solution.py:25
  286.1 10.6 %collective-permute-start = (bf16[8,16,512]{2,1,0:T(8,128)(2,1)S(1)}, bf16[8,16,512]{2,1,0:T(8,128)(2,1)S(1)}, u32[]{:S(2)}, u32[]{:S(2)}) collective-permute-start(bf16[8,16,512]{2,1,0:T(8,128)(2,1)S(1)} %get-tuple-element.201), channel_id=1, source_target_pairs={{31,0},{0,1},{1,2},{2,3},{3,4},{4,5},{5,6},{6,7},{7,8},{8,9},{9,10... | collective-permute-start | bytes 393224 | tf_op jit(solution)/shard_map/while/body/eval_jaxpr/ppermute | solution.py:25
  297.8 10.6 %collective-permute-start = (bf16[8,16,512]{2,1,0:T(8,128)(2,1)S(1)}, bf16[8,16,512]{2,1,0:T(8,128)(2,1)S(1)}, u32[]{:S(2)}, u32[]{:S(2)}) collective-permute-start(bf16[8,16,512]{2,1,0:T(8,128)(2,1)S(1)} %get-tuple-element.201), channel_id=1, source_target_pairs={{31,0},{0,1},{1,2},{2,3},{3,4},{4,5},{5,6},{6,7},{7,8},{8,9},{9,10... | collective-permute-start | bytes 393224 | tf_op jit(solution)/shard_map/while/body/eval_jaxpr/ppermute | solution.py:25
  309.5 10.6 %collective-permute-start = (bf16[8,16,512]{2,1,0:T(8,128)(2,1)S(1)}, bf16[8,16,512]{2,1,0:T(8,128)(2,1)S(1)}, u32[]{:S(2)}, u32[]{:S(2)}) collective-permute-start(bf16[8,16,512]{2,1,0:T(8,128)(2,1)S(1)} %get-tuple-element.201), channel_id=1, source_target_pairs={{31,0},{0,1},{1,2},{2,3},{3,4},{4,5},{5,6},{6,7},{7,8},{8,9},{9,10... | collective-permute-start | bytes 393224 | tf_op jit(solution)/shard_map/while/body/eval_jaxpr/ppermute | solution.py:25
  321.2 10.6 %collective-permute-start = (bf16[8,16,512]{2,1,0:T(8,128)(2,1)S(1)}, bf16[8,16,512]{2,1,0:T(8,128)(2,1)S(1)}, u32[]{:S(2)}, u32[]{:S(2)}) collective-permute-start(bf16[8,16,512]{2,1,0:T(8,128)(2,1)S(1)} %get-tuple-element.201), channel_id=1, source_target_pairs={{31,0},{0,1},{1,2},{2,3},{3,4},{4,5},{5,6},{6,7},{7,8},{8,9},{9,10... | collective-permute-start | bytes 393224 | tf_op jit(solution)/shard_map/while/body/eval_jaxpr/ppermute | solution.py:25
  332.9 10.6 %collective-permute-start = (bf16[8,16,512]{2,1,0:T(8,128)(2,1)S(1)}, bf16[8,16,512]{2,1,0:T(8,128)(2,1)S(1)}, u32[]{:S(2)}, u32[]{:S(2)}) collective-permute-start(bf16[8,16,512]{2,1,0:T(8,128)(2,1)S(1)} %get-tuple-element.201), channel_id=1, source_target_pairs={{31,0},{0,1},{1,2},{2,3},{3,4},{4,5},{5,6},{6,7},{7,8},{8,9},{9,10... | collective-permute-start | bytes 393224 | tf_op jit(solution)/shard_map/while/body/eval_jaxpr/ppermute | solution.py:25
  344.6 10.6 %collective-permute-start = (bf16[8,16,512]{2,1,0:T(8,128)(2,1)S(1)}, bf16[8,16,512]{2,1,0:T(8,128)(2,1)S(1)}, u32[]{:S(2)}, u32[]{:S(2)}) collective-permute-start(bf16[8,16,512]{2,1,0:T(8,128)(2,1)S(1)} %get-tuple-element.201), channel_id=1, source_target_pairs={{31,0},{0,1},{1,2},{2,3},{3,4},{4,5},{5,6},{6,7},{7,8},{8,9},{9,10... | collective-permute-start | bytes 393224 | tf_op jit(solution)/shard_map/while/body/eval_jaxpr/ppermute | solution.py:25
  356.2 10.6 %collective-permute-start = (bf16[8,16,512]{2,1,0:T(8,128)(2,1)S(1)}, bf16[8,16,512]{2,1,0:T(8,128)(2,1)S(1)}, u32[]{:S(2)}, u32[]{:S(2)}) collective-permute-start(bf16[8,16,512]{2,1,0:T(8,128)(2,1)S(1)} %get-tuple-element.201), channel_id=1, source_target_pairs={{31,0},{0,1},{1,2},{2,3},{3,4},{4,5},{5,6},{6,7},{7,8},{8,9},{9,10... | collective-permute-start | bytes 393224 | tf_op jit(solution)/shard_map/while/body/eval_jaxpr/ppermute | solution.py:25
  367.9 10.6 %collective-permute-start = (bf16[8,16,512]{2,1,0:T(8,128)(2,1)S(1)}, bf16[8,16,512]{2,1,0:T(8,128)(2,1)S(1)}, u32[]{:S(2)}, u32[]{:S(2)}) collective-permute-start(bf16[8,16,512]{2,1,0:T(8,128)(2,1)S(1)} %get-tuple-element.201), channel_id=1, source_target_pairs={{31,0},{0,1},{1,2},{2,3},{3,4},{4,5},{5,6},{6,7},{7,8},{8,9},{9,10... | collective-permute-start | bytes 393224 | tf_op jit(solution)/shard_map/while/body/eval_jaxpr/ppermute | solution.py:25
  379.6 10.6 %collective-permute-start = (bf16[8,16,512]{2,1,0:T(8,128)(2,1)S(1)}, bf16[8,16,512]{2,1,0:T(8,128)(2,1)S(1)}, u32[]{:S(2)}, u32[]{:S(2)}) collective-permute-start(bf16[8,16,512]{2,1,0:T(8,128)(2,1)S(1)} %get-tuple-element.201), channel_id=1, source_target_pairs={{31,0},{0,1},{1,2},{2,3},{3,4},{4,5},{5,6},{6,7},{7,8},{8,9},{9,10... | collective-permute-start | bytes 393224 | tf_op jit(solution)/shard_map/while/body/eval_jaxpr/ppermute | solution.py:25
  391.3 10.6 %collective-permute-start = (bf16[8,16,512]{2,1,0:T(8,128)(2,1)S(1)}, bf16[8,16,512]{2,1,0:T(8,128)(2,1)S(1)}, u32[]{:S(2)}, u32[]{:S(2)}) collective-permute-start(bf16[8,16,512]{2,1,0:T(8,128)(2,1)S(1)} %get-tuple-element.201), channel_id=1, source_target_pairs={{31,0},{0,1},{1,2},{2,3},{3,4},{4,5},{5,6},{6,7},{7,8},{8,9},{9,10... | collective-permute-start | bytes 393224 | tf_op jit(solution)/shard_map/while/body/eval_jaxpr/ppermute | solution.py:25
  402.9 10.6 %collective-permute-start = (bf16[8,16,512]{2,1,0:T(8,128)(2,1)S(1)}, bf16[8,16,512]{2,1,0:T(8,128)(2,1)S(1)}, u32[]{:S(2)}, u32[]{:S(2)}) collective-permute-start(bf16[8,16,512]{2,1,0:T(8,128)(2,1)S(1)} %get-tuple-element.201), channel_id=1, source_target_pairs={{31,0},{0,1},{1,2},{2,3},{3,4},{4,5},{5,6},{6,7},{7,8},{8,9},{9,10... | collective-permute-start | bytes 393224 | tf_op jit(solution)/shard_map/while/body/eval_jaxpr/ppermute | solution.py:25
  414.6 10.6 %collective-permute-start = (bf16[8,16,512]{2,1,0:T(8,128)(2,1)S(1)}, bf16[8,16,512]{2,1,0:T(8,128)(2,1)S(1)}, u32[]{:S(2)}, u32[]{:S(2)}) collective-permute-start(bf16[8,16,512]{2,1,0:T(8,128)(2,1)S(1)} %get-tuple-element.201), channel_id=1, source_target_pairs={{31,0},{0,1},{1,2},{2,3},{3,4},{4,5},{5,6},{6,7},{7,8},{8,9},{9,10... | collective-permute-start | bytes 393224 | tf_op jit(solution)/shard_map/while/body/eval_jaxpr/ppermute | solution.py:25
  (8 other events, 61.7 us)
where the time goes:
time: 447 us; the launch traced here: 444 us
  waiting for transfers between devices  280 us (63%)
  starting transfers between devices  78.3 us (18%)
  local copies, waits for them, and re-layouts  54.5 us (12%)
  other arithmetic  21.9 us (5%)
  matrix products  6.45 us (1%)
    ppermute x31, waiting for transfers between devices, shifted(): return lax.ppermute(block, axis, route)  273 us
    ppermute x31, starting transfers between devices, shifted(): return lax.ppermute(block, axis, route)  59.5 us
    dynamic_update_slice x32, local copies, waits for them, and re-layouts, insert_block(): lax.dynamic_update_slice(stacked_sum, result_block, (anchor, anchor, anch...  22.4 us
    another operation x4, other arithmetic  15.1 us
    ppermute x2, starting transfers between devices, from_behind(): return lax.ppermute(x, axis, pairs)  12.7 us
    unnamed x17, local copies, waits for them, and re-layouts  12.1 us
  transfers between devices with their start and end apart: 34, of which 32 were waited for; matrix products, arithmetic and copies ran while one was open for 1% of the time, Pallas kernels for 0%

commit v1 on v0

--- a/solution.py
+++ b/solution.py
@@ -2,6 +2,7 @@
 
 import jax
 import jax.numpy as jnp
+import numpy as np
 from jax import lax
 from jax.sharding import PartitionSpec as P
 
@@ -26,10 +27,11 @@
 
 
 def build_table():
-    sample_ids = jnp.arange(L, dtype=jnp.int32)[:, None]
-    bin_ids = (K0 + jnp.arange(F, dtype=jnp.int32))[None, :]
-    turns = (sample_ids * bin_ids % L).astype(jnp.float32) * jnp.float32(2.0 * math.pi / L)
-    return jnp.stack([jnp.cos(turns), -jnp.sin(turns)], axis=1).astype(jnp.bfloat16)
+    sample_ids = np.arange(L, dtype=np.int64)[:, None]
+    bin_ids = (K0 + np.arange(F, dtype=np.int64))[None, :]
+    turns = (sample_ids * bin_ids % L).astype(np.float32) * np.float32(2.0 * math.pi / L)
+    table = np.stack([np.cos(turns), -np.sin(turns)], axis=1)
+    return jnp.asarray(table.astype(jnp.bfloat16))
 
 
 def build_kernel():
@@ -89,34 +91,13 @@
     )
     left_side = jnp.concatenate([owned, flipped], axis=1)
 
-    def pair_block(visiting):
-        product = lax.dot_general(
-            left_side, visiting, (((2,), (2,)), ((0,), (0,))), preferred_element_type=jnp.float32
-        )
-        return (
-            jnp.transpose(product.reshape(own_bins, 2, per_group, per_group), (1, 0, 2, 3))
-            / window_total
-        )
-
-    chan_count = lax.axis_size("chan")
-    my_group = lax.axis_index("chan")
-    anchor = jnp.int32(0)
-
-    def insert_block(stacked_sum, result_block, source_group):
-        return lax.dynamic_update_slice(
-            stacked_sum, result_block, (anchor, anchor, anchor, source_group * per_group)
-        )
-
-    stacked_sum = jnp.zeros((2, own_bins, per_group, per_group * chan_count), jnp.float32)
-    stacked_sum = insert_block(stacked_sum, pair_block(owned), my_group)
-
-    def advance(turn_index, state_pair):
-        visiting, running = state_pair
-        visiting = shifted(visiting, "chan", 1)
-        source_group = (my_group - turn_index) % chan_count
-        return (visiting, insert_block(running, pair_block(visiting), source_group))
-
-    _, stacked_sum = lax.fori_loop(1, chan_count, advance, (owned, stacked_sum))
+    everyone = lax.all_gather(owned, "chan", axis=1, tiled=True)
+    product = lax.dot_general(
+        left_side, everyone, (((2,), (2,)), ((0,), (0,))), preferred_element_type=jnp.float32
+    )
+    stacked_sum = (
+        jnp.transpose(product.reshape(own_bins, 2, per_group, -1), (1, 0, 2, 3)) / window_total
+    )
     return (stored, stacked_sum)
 
 

time: 447 us -> 146 us (0.33)
  the two profiles are of different devices: /device:TPU:8 before, /device:TPU:1 now
where the time goes in v1:
time: 146 us; the launch traced here: 145 us
  waiting for transfers between devices  58.6 us (40%)
  local copies, waits for them, and re-layouts  22.8 us (16%)
  blocking collectives  20.3 us (14%)
  other arithmetic  18.1 us (12%)
  between operations  14.3 us (10%)
  starting transfers between devices  6.75 us (5%)
  matrix products  4.31 us (3%)
    all_gather x1, waiting for transfers between devices, on_device(): everyone = lax.all_gather(owned, 'chan', axis=1, tiled=True)  57.9 us
    all_to_all x1, blocking collectives, on_device(): lax.all_to_all(stored, 'tm', split_axis=0, concat_axis=2, tiled=True)  20.3 us
    another operation x3, other arithmetic  10.1 us
    ppermute x2, starting transfers between devices, from_behind(): return lax.ppermute(x, axis, pairs)  6.71 us
    another operation x6, local copies, waits for them, and re-layouts  3.98 us
    dot_general x1, matrix products, on_device(): lax.dot_general(left_side, everyone, (((2,), (2,)), ((0,), (0,))), prefer...  3.49 us
    unnamed x11, local copies, waits for them, and re-layouts  3.26 us
  transfers between devices with their start and end apart: 3, of which 2 were waited for; matrix products, arithmetic and copies ran while one was open for 6% of the time, Pallas kernels for 0%

profile of v1, /device:TPU:1, one launch (start us, length us, event | category | flops | bytes accessed | tf_op | source)
XLA Modules:
  0.0 145.1 jit_solution(12064245943709206517)
XLA Ops:
  7.2 0.8 slice.49
  8.0 1.3 collective-permute-start.1
  9.3 0.8 slice.48
  10.1 5.4 %collective-permute-start = (bf16[16,250]{1,0:T(8,128)(2,1)S(1)}, bf16[16,250]{1,0:T(8,128)(2,1)S(1)}, u32[]{:S(2)}, u32[]{:S(2)}) collective-permute-start(bf16[16,250]{1,0:T(8,128)(2,1)S(1)} %slice.48), channel_id=1, source_target_pairs={{0,32},{32,64},{64,96},{96,128},{128,160},{160,192},{192,224},{224... | collective-permute-start | bytes 24008 | tf_op jit(solution)/shard_map/ppermute | solution.py:20
  15.6 0.6 collective-permute-done
  16.3 1.5 %concatenate.12 = bf16[16,17500]{1,0:T(8,128)(2,1)S(1)} concatenate(bf16[16,250]{1,0:T(8,128)(2,1)S(1)} %collective-permute-done, bf16[16,16000]{1,0:T(8,128)(2,1)} %param.2, bf16[16,1250]{1,0:T(8,128)(2,1)S(1)} %collective-permute-done.1), dimensions={1} | concatenate | bytes 1120000 | tf_op jit(solution)/shard_map/concatenate | solution.py:73
  17.9 1.5 %reshape.45 = f32[16,69,2,128]{3,2,1,0:T(2,128)} reshape(f32[16,17664]{1,0:T(8,128)S(1)} %pad.5) | data formatting | bytes 2260992 | tf_op jit(solution)/shard_map/reshape
  19.5 1.3 copy.8
  20.8 9.6 %reduce-window.6 = f32[16,69,2,128]{3,1,2,0:T(8,128)S(1)} reduce-window(f32[16,69,2,128]{3,1,2,0:T(8,128)S(1)} %copy.8, f32[]{:T(128)} %constant.9.clone.1), window={size=1x1x1x128 pad=0_0x0_0x0_0x127_0}, to_apply=%region_0.1 | reduce-window | flops 35893248 | bytes 2260996 | tf_op jit(solution)/shard_map/reduce-window
  30.8 0.4 copy.9
  31.8 0.6 copy.12
  32.3 0.6 copy.11
  32.9 1.1 convert_element_type.11
  34.1 1.9 %reduce_window_sum.32 = f32[16,69,256]{2,0,1:T(8,128)} reshape(f32[16,69,2,128]{3,2,0,1:T(2,128)S(1)} %copy.12) | data formatting | bytes 2260992 | tf_op jit(solution)/shard_map/reduce_window_sum
  35.9 1.6 %slice_subtract_fusion = f32[16,69,1]{2,0,1:T(8,128)S(1)} fusion(f32[16,69,256]{2,0,1:T(8,128)} %reduce_window_sum.32), kind=kOutput, calls=%fused_computation.14 | output fusion | flops 76176 | bytes 1134912 | tf_op jit(solution)/shard_map/jit(cumsum)/reduce_window_sum | solution.py:52
  38.4 0.9 reduce_window_sum.31
  39.6 1.2 copy-done
  40.7 0.9 fusion.4
  41.6 1.1 reshape.47
  43.0 1.0 copy-done.3
  44.0 0.5 convolution_bitcast_fusion
  44.9 0.4 copy.14
  45.3 0.5 reshape.55
  45.9 20.3 %all_to_all.18 = bf16[16,2,2048]{2,1,0:T(2,128)(2,1)S(1)} all-to-all(bf16[16,2,2048]{2,1,0:T(2,128)(2,1)S(1)} %reshape.55), channel_id=1, replica_groups=mesh['tm'=16,'chan'=32] {'tm'}, dimensions={0} | all-to-all | bytes 262144 | tf_op jit(solution)/shard_map/all_to_all | solution.py:84
  66.7 1.1 all_to_all.16
  68.3 1.9 %fusion.26 = (bf16[8,16,16,1,16]{4,3,1,0,2:T(2,128)(2,1)S(1)}, bf16[8,16,16,1,16]{4,3,1,0,2:T(2,128)(2,1)S(1)}) fusion(bf16[8,16,16,2,16]{4,3,1,0,2:T(2,128)(2,1)S(1)} %reshape.49), kind=kLoop, calls=%fused_computation.40 | loop fusion | bytes 262144 | tf_op jit(solution)/shard_map/slice | solution.py:89
  70.2 1.1 copy_negate_fusion
  71.4 2.8 %pad_maximum_fusion = bf16[8,16,16,2,16]{4,3,2,1,0:T(2,128)(2,1)S(1)} fusion(bf16[8,16,16,1,16]{4,3,2,1,0:T(2,128)(2,1)S(1)} %copy_negate_fusion, bf16[8,16,16,1,16]{4,3,1,0,2:T(2,128)(2,1)S(1)} %get-tuple-element.2), kind=kLoop, calls=%fused_computation.11 | loop fusion | flops 262144 | bytes 262144 | tf_op jit(solution)/shard_map/stack | solution.py:89
  74.2 1.8 %reshape.50 = bf16[8,16,512]{2,1,0:T(8,128)(2,1)S(1)} reshape(bf16[8,16,16,2,16]{4,3,2,1,0:T(2,128)(2,1)S(1)} %pad_maximum_fusion) | data formatting | bytes 262144 | tf_op jit(solution)/shard_map/reshape | solution.py:89
  76.0 57.9 %all-gather.2.cloned.1.call-done = bf16[8,512,512]{2,1,0:T(8,128)(2,1)} async-done(((bf16[8,16,512]{2,1,0:T(8,128)(2,1)}), bf16[8,512,512]{2,1,0:T(8,128)(2,1)}) %all-gather.2.cloned.1.call-update) | async-done | bytes 4194320 | tf_op jit(solution)/shard_map/all_gather | solution.py:94
  133.9 3.5 %convolution_multiply_fusion = f32[8,32,512]{2,1,0:T(8,128)S(1)} fusion(bf16[8,512,512]{2,1,0:T(8,128)(2,1)} %all-gather.2.cloned.1.call-done, bf16[8,16,512]{2,1,0:T(8,128)(2,1)S(1)} %reshape.50, bf16[8,16,512]{2,1,0:T(8,128)(2,1)S(1)} %copy-done.1), kind=kOutput, calls=%fused_computation | convolution fusion | flops 134873088 | bytes 4980736 | tf_op jit(solution)/shard_map/dot_general | solution.py:95
  137.4 0.9 copy.27
  (30 shorter events, 3.9 us)
Async XLA Ops:
  7.2 126.7 %all-gather.2.cloned.1.call-start = ((), (), s32[]{:S(2)}) async-start(), calls=%async_computation.1 | async-start | bytes 4325376 | tf_op jit(solution)/shard_map/all_gather | solution.py:94
  8.0 8.3 %collective-permute-start.1 = (bf16[16,1250]{1,0:T(8,128)(2,1)S(1)}, bf16[16,1250]{1,0:T(8,128)(2,1)S(1)}, u32[]{:S(2)}, u32[]{:S(2)}) collective-permute-start(bf16[16,1250]{1,0:T(8,128)(2,1)S(1)} %slice.49), channel_id=1, source_target_pairs={{32,0},{64,32},{96,64},{128,96},{160,128},{192,160},{224,192},{256... | collective-permute-start | bytes 120008 | tf_op jit(solution)/shard_map/ppermute | solution.py:20
  10.1 6.2 %collective-permute-start = (bf16[16,250]{1,0:T(8,128)(2,1)S(1)}, bf16[16,250]{1,0:T(8,128)(2,1)S(1)}, u32[]{:S(2)}, u32[]{:S(2)}) collective-permute-start(bf16[16,250]{1,0:T(8,128)(2,1)S(1)} %slice.48), channel_id=1, source_target_pairs={{0,32},{32,64},{64,96},{96,128},{128,160},{160,192},{192,224},{224... | collective-permute-start | bytes 24008 | tf_op jit(solution)/shard_map/ppermute | solution.py:20
  39.5 1.3 copy-start
  42.7 1.2 copy-start.3
  44.9 21.8 %copy-start.2 = (bf16[128,16,2,16]{0,3,2,1:T(8,128)(2,1)}, bf16[128,16,2,16]{0,3,2,1:T(8,128)(2,1)S(1)}, u32[]{:S(2)}) copy-start(bf16[128,16,2,16]{0,3,2,1:T(8,128)(2,1)S(1)} %multiply_convert_fusion) | copy-start | bytes 393220
  74.2 59.7 %copy-start.1 = (bf16[8,16,512]{2,1,0:T(8,128)(2,1)S(1)}, bf16[8,16,512]{2,1,0:T(8,128)(2,1)}, u32[]{:S(2)}) copy-start(bf16[8,16,512]{2,1,0:T(8,128)(2,1)} %all_to_all.16) | copy-start | bytes 393220
Sparse Core Ops, SparseCore 0:
  68.0 65.8 all-gather.1

commit v2 on v1

v2 whole, which is shorter than its diff:
```python
import functools
import math

import jax
import jax.numpy as jnp
import numpy as np
from jax import lax
from jax.experimental import pallas as pl
from jax.experimental.pallas import tpu as pltpu
from jax.sharding import PartitionSpec as P

L = 2000
F = 128
K0 = 8
RM = 250
SMOOTH = 16
HOP = 1000
CD = 16
WD = 16
LEAD = 256
TAIL = 1280
NBLK = 67
KP = 1024
Q = 2
MESH = pl.DeviceIdType.MESH


def bin_order():
    return (np.arange(32)[None, :] * 4 + np.arange(4)[:, None]).reshape(-1)


def build_table():
    sample_ids = np.arange(L, dtype=np.int64)[:, None]
    bin_ids = (K0 + np.arange(F, dtype=np.int64))[None, :]
    turns = (sample_ids * bin_ids % L).astype(np.float32) * np.float32(2.0 * math.pi / L)
    both = np.stack([np.cos(turns), -np.sin(turns)], axis=0)
    both = both[:, :, bin_order()].transpose(0, 2, 1).reshape(2 * F, 2, HOP)
    out = np.zeros((2, 2 * F, KP), np.float32)
    out[:, :, :HOP] = both.transpose(1, 0, 2)
    return jnp.asarray(out.astype(jnp.bfloat16))


def build_kernel():
    positions = np.arange(F, dtype=np.float32)
    distance = positions[:, None] - positions[None, :]
    weights = np.exp(-distance * distance / np.float32(2.0 * SMOOTH * SMOOTH))
    weights = weights / np.sum(weights, axis=1, keepdims=True, dtype=np.float32)
    order = bin_order()
    return jnp.asarray(weights[order][:, order].astype(np.float32))


def build_band():
    i = np.arange(3 * 256)[:, None]
    j = np.arange(256)[None, :]
    first = LEAD - RM
    band = (i - j >= first) & (i - j <= first + 2 * RM)
    return jnp.asarray(band.astype(np.float32).astype(jnp.bfloat16))


def build_swap():
    out = np.zeros((256, 256), np.float32)
    for w in range(WD):
        for c in range(CD):
            out[w * CD + c, c * WD + w] = 1.0
    return jnp.asarray(out.astype(jnp.bfloat16))


def front_kernel(raw, lead, tail, table, kern, band, swap, stored, packed, ext, norm, pieces, mid):
    for i in range(62):
        ext[1 + i] = raw[:, 256 * i : 256 * i + 256]
    ext[0] = lead[...]
    ext[63, :, 0:128] = raw[:, 15872:16000]
    ext[63, :, 128:256] = tail[:, 0:128]
    for j in range(4):
        ext[64 + j] = tail[:, 128 + 256 * j : 384 + 256 * j]
    ext[68, :, 0:128] = tail[:, 1152:1280]
    ext[68, :, 128:256] = jnp.zeros((CD, 128), jnp.bfloat16)

    box = jnp.zeros((NBLK * CD, 256), jnp.float32)
    for d in range(3):
        box += jnp.dot(
            jnp.abs(ext[d : d + NBLK]).reshape(NBLK * CD, 256),
            band[256 * d : 256 * d + 256, :],
            preferred_element_type=jnp.float32,
        )
    inner = ext[1 : 1 + NBLK].reshape(NBLK * CD, 256).astype(jnp.float32)
    value = inner / (box * jnp.float32(1.0 / (2 * RM + 1)) + jnp.float32(1e-6))
    for i in range(NBLK):
        norm[:, 256 * i : 256 * i + 256] = value[CD * i : CD * i + CD, :]
    for p in range(WD + 1):
        start = p * HOP // 128 * 128
        off = p * HOP - start
        wide = norm[:, start : start + 1152]
        if off:
            wide = pltpu.roll(wide, 1152 - off, 1)
        pieces[CD * p : CD * p + CD, :] = wide[:, :KP].astype(jnp.bfloat16)

    contract = (((1,), (1,)), ((), ()))
    spec = lax.dot_general(
        table[0], pieces[0 : WD * CD, :], contract, preferred_element_type=jnp.float32
    ) + lax.dot_general(
        table[1], pieces[CD : CD + WD * CD, :], contract, preferred_element_type=jnp.float32
    )
    energy = spec[:F] * spec[:F] + spec[F:] * spec[F:]
    smoothed = jnp.dot(
        kern[...], energy, precision=lax.Precision.HIGHEST, preferred_element_type=jnp.float32
    )
    scale = lax.rsqrt(smoothed + jnp.float32(1e-6))
    white = (spec * jnp.concatenate([scale, scale], axis=0)).astype(jnp.bfloat16)
    turned = jnp.dot(white, swap[...], preferred_element_type=jnp.float32)
    group = lax.broadcasted_iota(jnp.int32, (32, 128), 1) // 16
    for hi in range(2):
        parts = []
        for b in range(4):
            for r in range(2):
                part = turned[r * F + b * 32 : r * F + b * 32 + 32, hi * 128 : hi * 128 + 128]
                slot = 2 * b + r
                parts.append(pltpu.roll(part, 16 * slot, 1) if slot else part)
        for lo in range(8):
            ch = hi * 8 + lo
            line = parts[0]
            for slot in range(1, 8):
                line = jnp.where(group == (lo + slot) % 8, parts[slot], line)
            if lo:
                line = pltpu.roll(line, 128 - 16 * lo, 1)
            mid[pl.ds(ch, 32, stride=CD), :] = line
    everything = mid[...]
    packed[...] = everything.reshape(32, CD, 128).astype(jnp.bfloat16)
    for b in range(4):
        turned_b = pltpu.roll(everything, 128 - 32 * b, 1) if b else everything
        stored[:, b] = turned_b[:, :32].reshape(32, CD, 32).astype(jnp.bfloat16)


def front(raw, lead, tail):
    vm = pl.BlockSpec(memory_space=pltpu.VMEM)
    return pl.pallas_call(
        front_kernel,
        out_shape=(
            jax.ShapeDtypeStruct((32, 4, CD, 32), jnp.bfloat16),
            jax.ShapeDtypeStruct((32, CD, 128), jnp.bfloat16),
        ),
        in_specs=[vm] * 7,
        out_specs=(vm, vm),
        scratch_shapes=[
            pltpu.VMEM((NBLK + 2, CD, 256), jnp.bfloat16),
            pltpu.VMEM((CD, 17280), jnp.float32),
            pltpu.VMEM((CD * (WD + 1), KP), jnp.bfloat16),
            pltpu.VMEM((512, 128), jnp.float32),
        ],
        compiler_params=pltpu.CompilerParams(vmem_limit_bytes=48 * 1024 * 1024),
        name="front",
    )(raw, lead, tail, build_table(), build_kernel(), build_band(), build_swap())


def gather_kernel(packed, out, local_sem, s1, r1, sy, ry, sx, rx, sp, rp):
    t = lax.axis_index("tm")
    c = lax.axis_index("chan")
    h, x, k = c // 8, (c // 2) % 4, c % 2

    def at(dh, dx):
        return ((h + dh) % 4) * 8 + ((x + dx) % 4) * 2 + k

    partner = c + 1 - 2 * k
    barrier = pltpu.get_barrier_semaphore()
    for d in range(1, 16):
        pl.semaphore_signal(barrier, inc=1, device_id=((t + d) % 16, c), device_id_type=MESH)
    for other in (at(1, 0), at(3, 0), at(0, 1), at(0, 3), partner):
        pl.semaphore_signal(barrier, inc=1, device_id=(t, other), device_id_type=MESH)
    pl.semaphore_wait(barrier, 20)

    mine = pltpu.make_async_copy(packed.at[t], out.at[c, :, t], local_sem)
    mine.start()
    first = []
    for d in range(1, 16):
        peer = (t + d) % 16
        copy = pltpu.make_async_remote_copy(
            src_ref=packed.at[peer],
            dst_ref=out.at[c, :, t],
            send_sem=s1.at[d],
            recv_sem=r1.at[d],
            device_id=(peer, c),
            device_id_type=MESH,
        )
        copy.start()
        first.append(copy)
    mine.wait()
    for copy in first:
        copy.wait_recv()

    sent = []

    def send(dh, dx, q, to, send_sem, recv_sem):
        block = at(dh, dx)
        copy = pltpu.make_async_remote_copy(
            src_ref=out.at[block, q],
            dst_ref=out.at[block, q],
            send_sem=send_sem,
            recv_sem=recv_sem,
            device_id=(t, to),
            device_id_type=MESH,
        )
        copy.start()
        sent.append(copy)

    def landed(dh, dx, q, sem):
        block = out.at[at(dh, dx), q]
        pltpu.make_async_copy(block, block, sem).wait()

    def along_x(dh, q):
        send(dh, 0, q, at(0, 1), sx.at[dh, 0, q], rx.at[dh, 2, q])
        send(dh, 0, q, at(0, 3), sx.at[dh, 1, q], rx.at[dh, 0, q])

    def to_partner(dh, dx, q):
        send(dh, dx, q, partner, sp.at[dh, dx, q], rp.at[dh, dx, q])

    def own(q):
        send(0, 0, q, at(1, 0), sy.at[0, q], ry.at[2, q])
        send(0, 0, q, at(3, 0), sy.at[1, q], ry.at[0, q])
        along_x(0, q)
        to_partner(0, 0, q)

    def from_y(dh, q):
        landed(dh, 0, q, ry.at[dh - 1, q])
        if dh == 3 and q == 0:
            send(3, 0, 0, at(1, 0), sy.at[2, 0], ry.at[1, 0])
        if dh == 1 and q == 1:
            send(1, 0, 1, at(3, 0), sy.at[2, 1], ry.at[1, 1])
        along_x(dh, q)
        to_partner(dh, 0, q)

    def from_x(dh, dx, q):
        landed(dh, dx, q, rx.at[dh, dx - 1, q])
        if dx == 3 and q == 0:
            send(dh, 3, 0, at(0, 1), sx.at[dh, 2, 0], rx.at[dh, 1, 0])
        if dx == 1 and q == 1:
            send(dh, 1, 1, at(0, 3), sx.at[dh, 2, 1], rx.at[dh, 1, 1])
        to_partner(dh, dx, q)

    own(0)
    own(1)
    from_x(0, 3, 0)
    from_x(0, 1, 0)
    from_y(3, 0)
    from_y(1, 0)
    from_x(0, 3, 1)
    from_x(0, 1, 1)
    from_y(3, 1)
    from_y(1, 1)
    from_x(0, 2, 0)
    from_x(0, 2, 1)
    for dh in (3, 1):
        from_x(dh, 3, 0)
        from_x(dh, 1, 0)
    from_y(2, 0)
    from_y(2, 1)
    for dh in (3, 1):
        from_x(dh, 3, 1)
        from_x(dh, 1, 1)
    for dh in (3, 1):
        from_x(dh, 2, 0)
        from_x(dh, 2, 1)
    from_x(2, 3, 0)
    from_x(2, 1, 0)
    from_x(2, 3, 1)
    from_x(2, 1, 1)
    from_x(2, 2, 0)
    from_x(2, 2, 1)
    for dh in range(4):
        for dx in range(4):
            for q in range(Q):
                block = out.at[((h + dh) % 4) * 8 + ((x + dx) % 4) * 2 + 1 - k, q]
                pltpu.make_async_copy(block, block, rp.at[dh, dx, q]).wait()
    for copy in first + sent:
        copy.wait_send()


def gather(packed):
    dma = pltpu.SemaphoreType.DMA
    return pl.pallas_call(
        gather_kernel,
        out_shape=jax.ShapeDtypeStruct((32, Q, 16, CD, 128), jnp.bfloat16),
        in_specs=[pl.BlockSpec(memory_space=pl.ANY)],
        out_specs=pl.BlockSpec(memory_space=pl.ANY),
        scratch_shapes=[
            dma(()),
            dma((16,)),
            dma((16,)),
            dma((3, 2)),
            dma((3, 2)),
            dma((4, 3, 2)),
            dma((4, 3, 2)),
            dma((4, 4, 2)),
            dma((4, 4, 2)),
        ],
        compiler_params=pltpu.CompilerParams(collective_id=0, has_side_effects=True),
        name="gather",
    )(packed)


def cross_kernel(mine, everyone, out):
    lane = lax.broadcasted_iota(jnp.int32, (CD, 128), 1)
    flip = (lane // 16) % 2
    total = jnp.zeros((2 * 4 * CD, 512), jnp.float32)
    for pair in range(8):
        lefts, rights = [], []
        for t in (2 * pair, 2 * pair + 1):
            joined = mine[0, 0, t].astype(jnp.float32)
            flipped = jnp.where(flip == 0, pltpu.roll(joined, 112, 1), -pltpu.roll(joined, 16, 1))
            rows = []
            for source in (joined, flipped):
                for b in range(4):
                    rows.append(jnp.where(lane // 32 == b, source, 0.0).astype(jnp.bfloat16))
            lefts.append(jnp.concatenate(rows, axis=0))
            rights.append(everyone[:, 0, t].reshape(512, 128))
        total += lax.dot_general(
            jnp.concatenate(lefts, axis=1),
            jnp.concatenate(rights, axis=1),
            (((1,), (1,)), ((), ())),
            preferred_element_type=jnp.float32,
        )
    out[...] = (total * jnp.float32(1.0 / 256.0)).reshape(2, 4, CD, 512)


def cross(everyone):
    mine = lax.dynamic_slice_in_dim(everyone, lax.axis_index("chan"), 1, 0)
    return pl.pallas_call(
        cross_kernel,
        grid=(Q,),
        out_shape=jax.ShapeDtypeStruct((2, 4 * Q, CD, 512), jnp.float32),
        in_specs=[
            pl.BlockSpec((1, 1, 16, CD, 128), lambda q: (0, q, 0, 0, 0)),
            pl.BlockSpec((32, 1, 16, CD, 128), lambda q: (0, q, 0, 0, 0)),
        ],
        out_specs=pl.BlockSpec((2, 4, CD, 512), lambda q: (0, q, 0, 0)),
        compiler_params=pltpu.CompilerParams(vmem_limit_bytes=40 * 1024 * 1024),
        name="cross",
    )(mine, everyone)


def from_behind(x, axis, by):
    count = lax.axis_size(axis)
    pairs = [(i, i + by) for i in range(count) if 0 <= i + by < count]
    return lax.ppermute(x, axis, pairs)


def on_device(raw):
    samples = raw.shape[1]
    lead = from_behind(raw[:, samples - LEAD :], "tm", 1)
    tail = from_behind(raw[:, :TAIL], "tm", -1)
    stored, packed = front(raw, lead, tail)
    everyone = gather(packed.reshape(16, Q, CD, 128))
    return stored.reshape(F, CD, 2 * WD), cross(everyone)


def solution(mesh):
    return jax.shard_map(
        on_device,
        mesh=mesh,
        in_specs=(P("chan", "tm"),),
        out_specs=(P(None, "chan", "tm"), P(None, "tm", "chan", None)),
        check_vma=False,
    )
```

time: 146 us -> 79 us (0.54)
  Pallas kernels: 0 us -> 59 us
  waiting for transfers between devices: 58.6 us -> 0.77 us
  blocking collectives: 20.3 us -> 0 us
  other arithmetic: 18.1 us -> 0 us
  between operations: 14.3 us -> 0.69 us
  local copies, waits for them, and re-layouts: 22.8 us -> 11.3 us
  matrix products: 4.31 us -> 0 us
    pallas_call x0 -> x3, Pallas kernels: none -> 59 us  [the longest x1 53.8 us: gather(): pl.pallas_call(gather_kernel, out_shape=jax.ShapeDtypeStruct((32, Q, 16,...]
    all_gather x1 -> x0, waiting for transfers between devices: 57.9 us -> none  [on_device(): everyone = lax.all_gather(owned, 'chan', axis=1, tiled=True)]
    all_to_all x1 -> x0, blocking collectives: 20.3 us -> none  [on_device(): lax.all_to_all(stored, 'tm', split_axis=0, concat_axis=2, tiled=True)]
    another operation x5 -> x0, other arithmetic: 14.5 us -> none
    reshape x6 -> x0, local copies, waits for them, and re-layouts: 6.61 us -> none
    unnamed x11 -> x15, local copies, waits for them, and re-layouts: 3.26 us -> 8.92 us
    another operation x6 -> x0, local copies, waits for them, and re-layouts: 3.98 us -> none
    dot_general x2 -> x0, matrix products: 3.96 us -> none  [the longest x1 3.49 us: on_device(): lax.dot_general(left_side, everyone, (((2,), (2,)), ((0,), (0,))), prefer...]
  transfers between devices with their start and end apart: 3 -> 2, of which waited for: 2 -> 1; matrix products, arithmetic and copies ran while one was open for 6% -> 1% of each run, Pallas kernels for 0% -> 0%
where the time goes in v2:
time: 79 us; the launch traced here: 78.5 us
  Pallas kernels  59 us (75%)
  local copies, waits for them, and re-layouts  11.3 us (14%)
  starting transfers between devices  6.71 us (8%)
    pallas_call x1, Pallas kernels, gather(): pl.pallas_call(gather_kernel, out_shape=jax.ShapeDtypeStruct((32, Q, 16,...  53.8 us
    unnamed x15, local copies, waits for them, and re-layouts  8.92 us
    ppermute x2, starting transfers between devices, from_behind(): return lax.ppermute(x, axis, pairs)  6.71 us
    pallas_call x1, Pallas kernels, cross(): pl.pallas_call(cross_kernel, grid=(Q,), out_shape=jax.ShapeDtypeStruct((2...  2.64 us
    pallas_call x1, Pallas kernels, front(): pl.pallas_call(front_kernel, out_shape=(jax.ShapeDtypeStruct((32, 4, CD,...  2.56 us
  transfers between devices with their start and end apart: 2, of which 1 were waited for; matrix products, arithmetic and copies ran while one was open for 1% of the time, Pallas kernels for 0%

profile of v2, /device:TPU:1, one launch (start us, length us, event | category | flops | bytes accessed | tf_op | source)
XLA Modules:
  0.0 78.5 jit_solution(14315134896540420060)
XLA Ops:
  0.6 0.8 slice.7
  1.4 1.3 %collective-permute-start.1 = (bf16[16,1280]{1,0:T(8,128)(2,1)S(1)}, bf16[16,1280]{1,0:T(8,128)(2,1)S(1)}, u32[]{:S(2)}, u32[]{:S(2)}) collective-permute-start(bf16[16,1280]{1,0:T(8,128)(2,1)S(1)} %slice.7), channel_id=1, source_target_pairs={{32,0},{64,32},{96,64},{128,96},{160,128},{192,160},{224,192},{256... | collective-permute-start | bytes 122888 | tf_op jit(solution)/shard_map/ppermute | solution.py:343
  2.7 0.7 slice.6
  3.4 5.4 %collective-permute-start = (bf16[16,256]{1,0:T(8,128)(2,1)S(1)}, bf16[16,256]{1,0:T(8,128)(2,1)S(1)}, u32[]{:S(2)}, u32[]{:S(2)}) collective-permute-start(bf16[16,256]{1,0:T(8,128)(2,1)S(1)} %slice.6), channel_id=1, source_target_pairs={{0,32},{32,64},{64,96},{96,128},{128,160},{160,192},{192,224},{224... | collective-permute-start | bytes 24584 | tf_op jit(solution)/shard_map/ppermute | solution.py:343
  8.8 0.8 collective-permute-done.lead
  9.6 0.0 collective-permute-done.1.tail
  9.6 0.0 copy-start.1
  9.6 1.2 %copy-done.1 = bf16[2,256,1024]{2,1,0:T(8,128)(2,1)S(1)} copy-done((bf16[2,256,1024]{2,1,0:T(8,128)(2,1)S(1)}, bf16[2,256,1024]{2,1,0:T(8,128)(2,1)}, u32[]{:S(2)}) %copy-start.1) | copy-done | bytes 1048600
  10.8 0.0 copy-start.2
  10.8 1.0 %copy-done.2 = bf16[16,16000]{1,0:T(8,128)(2,1)S(1)} copy-done((bf16[16,16000]{1,0:T(8,128)(2,1)S(1)}, bf16[16,16000]{1,0:T(8,128)(2,1)}, u32[]{:S(2)}) %copy-start.2) | copy-done | bytes 512024
  11.9 0.0 copy-start.3
  11.9 1.0 %copy-done.3 = bf16[768,256]{1,0:T(8,128)(2,1)S(1)} copy-done((bf16[768,256]{1,0:T(8,128)(2,1)S(1)}, bf16[768,256]{1,0:T(8,128)(2,1)}, u32[]{:S(2)}) %copy-start.3) | copy-done | bytes 393240
  12.9 0.0 copy-start.4
  12.9 0.9 %copy-done.4 = bf16[256,256]{1,0:T(8,128)(2,1)S(1)} copy-done((bf16[256,256]{1,0:T(8,128)(2,1)S(1)}, bf16[256,256]{1,0:T(8,128)(2,1)}, u32[]{:S(2)}) %copy-start.4) | copy-done | bytes 131096
  13.8 0.0 copy-start.6
  13.8 0.8 %copy-done.6 = f32[128,128]{1,0:T(8,128)S(1)} copy-done((f32[128,128]{1,0:T(8,128)S(1)}, f32[128,128]{1,0:T(8,128)}, u32[]{:S(2)}) %copy-start.6) | copy-done | bytes 65560
  14.6 2.6 %front.1 = (bf16[32,4,16,32]{3,2,1,0:T(8,128)(2,1)S(1)}, bf16[32,16,128]{2,1,0:T(8,128)(2,1)S(1)}) custom-call(bf16[16,16000]{1,0:T(8,128)(2,1)S(1)} %copy-done.2, bf16[16,256]{1,0:T(8,128)(2,1)S(1)} %collective-permute-done.lead, bf16[16,1280]{1,0:T(8,128)(2,1)S(1)} %collective-permute-done.1.tail, bf16[2,256,1024]{2,1,0:T(8,128)(2,1)S(1)} %copy-done.1, ...), custom_call_target="tpu_custom_call" | custom-call | tf_op jit(solution)/shard_map/front/pallas_call | solution.py:136
  17.2 0.0 copy-start.5
  17.2 0.6 copy-done.5
  17.9 1.1 %copy.7 = bf16[128,16,32]{0,2,1:T(8,128)(2,1)} copy(bf16[128,16,32]{2,1,0:T(8,128)(2,1)S(1)} %bitcast.2) | data formatting | bytes 262144
  18.9 53.8 %gather.1.everyone = bf16[32,2,16,16,128]{4,3,2,1,0:T(8,128)(2,1)} custom-call(bf16[16,2,16,128]{3,2,1,0:T(8,128)(2,1)} %bitcast.3), custom_call_target="tpu_custom_call" | custom-call | tf_op jit(solution)/shard_map/gather/pallas_call | solution.py:279
  72.7 0.9 %constant_dynamic-slice_fusion.mine = bf16[1,2,16,16,128]{4,3,2,1,0:T(8,128)(2,1)S(1)} fusion(bf16[32,2,16,16,128]{4,3,2,1,0:T(8,128)(2,1)} %gather.1.everyone, s32[]{:T(128)S(6)} %select_n.3), kind=kLoop, calls=%fused_computation | loop fusion | bytes 262148 | tf_op jit(solution)/shard_map/dynamic_slice | solution.py:325
  73.7 0.0 copy-start
  73.7 2.2 %copy-done = bf16[32,2,16,16,128]{4,3,2,1,0:T(8,128)(2,1)S(1)} copy-done((bf16[32,2,16,16,128]{4,3,2,1,0:T(8,128)(2,1)S(1)}, bf16[32,2,16,16,128]{4,3,2,1,0:T(8,128)(2,1)}, u32[]{:S(2)}) %copy-start) | copy-done | bytes 4194328
  75.8 2.6 %cross.1 = f32[2,8,16,512]{3,2,1,0:T(8,128)} custom-call(bf16[1,2,16,16,128]{4,3,2,1,0:T(8,128)(2,1)S(1)} %constant_dynamic-slice_fusion.mine, bf16[32,2,16,16,128]{4,3,2,1,0:T(8,128)(2,1)S(1)} %copy-done), custom_call_target="tpu_custom_call" | custom-call | tf_op jit(solution)/shard_map/cross/pallas_call | solution.py:326
Async XLA Ops:
  1.4 8.2 %collective-permute-start.1 = (bf16[16,1280]{1,0:T(8,128)(2,1)S(1)}, bf16[16,1280]{1,0:T(8,128)(2,1)S(1)}, u32[]{:S(2)}, u32[]{:S(2)}) collective-permute-start(bf16[16,1280]{1,0:T(8,128)(2,1)S(1)} %slice.7), channel_id=1, source_target_pairs={{32,0},{64,32},{96,64},{128,96},{160,128},{192,160},{224,192},{256... | collective-permute-start | bytes 122888 | tf_op jit(solution)/shard_map/ppermute | solution.py:343
  3.4 6.2 %collective-permute-start = (bf16[16,256]{1,0:T(8,128)(2,1)S(1)}, bf16[16,256]{1,0:T(8,128)(2,1)S(1)}, u32[]{:S(2)}, u32[]{:S(2)}) collective-permute-start(bf16[16,256]{1,0:T(8,128)(2,1)S(1)} %slice.6), channel_id=1, source_target_pairs={{0,32},{32,64},{64,96},{96,128},{128,160},{160,192},{192,224},{224... | collective-permute-start | bytes 24584 | tf_op jit(solution)/shard_map/ppermute | solution.py:343
  9.6 1.2 %copy-start.1 = (bf16[2,256,1024]{2,1,0:T(8,128)(2,1)S(1)}, bf16[2,256,1024]{2,1,0:T(8,128)(2,1)}, u32[]{:S(2)}) copy-start(bf16[2,256,1024]{2,1,0:T(8,128)(2,1)} %constant.16.clone.table) | copy-start | bytes 3145732
  10.8 1.0 %copy-start.2 = (bf16[16,16000]{1,0:T(8,128)(2,1)S(1)}, bf16[16,16000]{1,0:T(8,128)(2,1)}, u32[]{:S(2)}) copy-start(bf16[16,16000]{1,0:T(8,128)(2,1)} %raw.1) | copy-start | bytes 1536004
  11.9 1.0 %copy-start.3 = (bf16[768,256]{1,0:T(8,128)(2,1)S(1)}, bf16[768,256]{1,0:T(8,128)(2,1)}, u32[]{:S(2)}) copy-start(bf16[768,256]{1,0:T(8,128)(2,1)} %constant.18.clone.band) | copy-start | bytes 1179652
  12.9 0.9 %copy-start.4 = (bf16[256,256]{1,0:T(8,128)(2,1)S(1)}, bf16[256,256]{1,0:T(8,128)(2,1)}, u32[]{:S(2)}) copy-start(bf16[256,256]{1,0:T(8,128)(2,1)} %constant.19.clone.swap) | copy-start | bytes 393220
  13.8 0.8 %copy-start.6 = (f32[128,128]{1,0:T(8,128)S(1)}, f32[128,128]{1,0:T(8,128)}, u32[]{:S(2)}) copy-start(f32[128,128]{1,0:T(8,128)} %constant.17.clone.kern) | copy-start | bytes 196612
  17.2 0.7 copy-start.5
  73.7 2.2 %copy-start = (bf16[32,2,16,16,128]{4,3,2,1,0:T(8,128)(2,1)S(1)}, bf16[32,2,16,16,128]{4,3,2,1,0:T(8,128)(2,1)}, u32[]{:S(2)}) copy-start(bf16[32,2,16,16,128]{4,3,2,1,0:T(8,128)(2,1)} %gather.1.everyone) | copy-start | bytes 12582916

commit v3 on v1

v3 whole, which is shorter than its diff:
```python
import math

import jax
import jax.numpy as jnp
import numpy as np
from jax import lax
from jax.experimental import pallas as pl
from jax.experimental.pallas import tpu as pltpu
from jax.sharding import PartitionSpec as P

L = 2000
F = 128
K0 = 8
RM = 250
SMOOTH = 16
HOP = 1000
CD = 16
WD = 16
LEAD = 256
TAIL = 1280
NBLK = 67
KP = 1024
PAIRS = 64
MESH = pl.DeviceIdType.MESH


def bin_order():
    return (np.arange(PAIRS)[None, :] * 2 + np.arange(2)[:, None]).reshape(-1)


def build_table():
    sample_ids = np.arange(L, dtype=np.int64)[:, None]
    bin_ids = (K0 + np.arange(F, dtype=np.int64))[None, :]
    turns = (sample_ids * bin_ids % L).astype(np.float32) * np.float32(2.0 * math.pi / L)
    both = np.stack([np.cos(turns), -np.sin(turns)], axis=0)
    both = both[:, :, bin_order()].transpose(0, 2, 1).reshape(2 * F, 2, HOP)
    out = np.zeros((2, 2 * F, KP), np.float32)
    out[:, :, :HOP] = both.transpose(1, 0, 2)
    return jnp.asarray(out.astype(jnp.bfloat16))


def build_kernel():
    positions = np.arange(F, dtype=np.float32)
    distance = positions[:, None] - positions[None, :]
    weights = np.exp(-distance * distance / np.float32(2.0 * SMOOTH * SMOOTH))
    weights = weights / np.sum(weights, axis=1, keepdims=True, dtype=np.float32)
    order = bin_order()
    return jnp.asarray(weights[order][:, order].astype(np.float32))


def build_band():
    i = np.arange(3 * 256)[:, None]
    j = np.arange(256)[None, :]
    first = LEAD - RM
    band = (i - j >= first) & (i - j <= first + 2 * RM)
    return jnp.asarray(band.astype(np.float32).astype(jnp.bfloat16))


def build_swap():
    out = np.zeros((256, 256), np.float32)
    for w in range(WD):
        for c in range(CD):
            out[w * CD + c, c * WD + w] = 1.0
    return jnp.asarray(out.astype(jnp.bfloat16))


def front_kernel(
    raw_hbm, table_hbm, kern_hbm, band_hbm, swap_hbm, stored, packed,
    raw, lead, tail, table, kern, band, swap, ext, norm, pieces, mid, load_sem, halo_send, halo_recv
):
    t = lax.axis_index("tm")
    c = lax.axis_index("chan")
    loads = []
    for n, (src, dst) in enumerate(
        ((raw_hbm, raw), (band_hbm, band), (table_hbm, table), (kern_hbm, kern), (swap_hbm, swap))
    ):
        load = pltpu.make_async_copy(src, dst, load_sem.at[n])
        load.start()
        loads.append(load)
    after, before = (t + 1) % 16, (t + 15) % 16
    barrier = pltpu.get_barrier_semaphore()
    for other in (after, before):
        pl.semaphore_signal(barrier, inc=1, device_id=(other, c), device_id_type=MESH)
    pl.semaphore_wait(barrier, 2)
    halos = []
    for n, (first, count, dst, other) in enumerate(
        ((raw_hbm.shape[1] - LEAD, LEAD, lead, after), (0, TAIL, tail, before))
    ):
        halo = pltpu.make_async_remote_copy(
            src_ref=raw_hbm.at[:, first : first + count],
            dst_ref=dst,
            send_sem=halo_send.at[n],
            recv_sem=halo_recv.at[n],
            device_id=(other, c),
            device_id_type=MESH,
        )
        halo.start()
        halos.append(halo)
    loads[0].wait()
    for i in range(62):
        ext[1 + i] = raw[:, 256 * i : 256 * i + 256]
    ext[63, :, 0:128] = raw[:, 15872:16000]
    ext[68, :, 128:256] = jnp.zeros((CD, 128), jnp.bfloat16)
    for halo in halos:
        halo.wait_recv()
    has_lead = jnp.full((CD, LEAD), t, jnp.int32) > 0
    has_tail = jnp.full((CD, TAIL), t, jnp.int32) < 15
    ext[0] = jnp.where(has_lead, lead[...].astype(jnp.float32), 0.0).astype(jnp.bfloat16)
    behind = jnp.where(has_tail, tail[...].astype(jnp.float32), 0.0).astype(jnp.bfloat16)
    ext[63, :, 128:256] = behind[:, 0:128]
    for j in range(4):
        ext[64 + j] = behind[:, 128 + 256 * j : 384 + 256 * j]
    ext[68, :, 0:128] = behind[:, 1152:1280]
    for load in loads[1:]:
        load.wait()

    box = jnp.zeros((NBLK * CD, 256), jnp.float32)
    for d in range(3):
        box += jnp.dot(
            jnp.abs(ext[d : d + NBLK]).reshape(NBLK * CD, 256),
            band[256 * d : 256 * d + 256, :],
            preferred_element_type=jnp.float32,
        )
    inner = ext[1 : 1 + NBLK].reshape(NBLK * CD, 256).astype(jnp.float32)
    value = inner / (box * jnp.float32(1.0 / (2 * RM + 1)) + jnp.float32(1e-6))
    for i in range(NBLK):
        norm[:, 256 * i : 256 * i + 256] = value[CD * i : CD * i + CD, :]
    for p in range(WD + 1):
        start = p * HOP // 128 * 128
        off = p * HOP - start
        wide = norm[:, start : start + 1152]
        if off:
            wide = pltpu.roll(wide, 1152 - off, 1)
        pieces[CD * p : CD * p + CD, :] = wide[:, :KP].astype(jnp.bfloat16)

    contract = (((1,), (1,)), ((), ()))
    spec = lax.dot_general(
        table[0], pieces[0 : WD * CD, :], contract, preferred_element_type=jnp.float32
    ) + lax.dot_general(
        table[1], pieces[CD : CD + WD * CD, :], contract, preferred_element_type=jnp.float32
    )
    energy = spec[:F] * spec[:F] + spec[F:] * spec[F:]
    smoothed = jnp.dot(
        kern[...], energy, precision=lax.Precision.HIGHEST, preferred_element_type=jnp.float32
    )
    scale = lax.rsqrt(smoothed + jnp.float32(1e-6))
    white = (spec * jnp.concatenate([scale, scale], axis=0)).astype(jnp.bfloat16)
    turned = jnp.dot(white, swap[...], preferred_element_type=jnp.float32)
    group = lax.broadcasted_iota(jnp.int32, (PAIRS, 128), 1) // 16
    parts = []
    for b in range(2):
        for half in range(2):
            for r in range(2):
                row = r * F + b * PAIRS
                part = turned[row : row + PAIRS, half * 128 : half * 128 + 128]
                slot = len(parts)
                parts.append(pltpu.roll(part, 16 * slot, 1) if slot else part)
    for ih in range(8):
        line = parts[0]
        for slot in range(1, 8):
            line = jnp.where(group == (ih + slot) % 8, parts[slot], line)
        if ih:
            line = pltpu.roll(line, 128 - 16 * ih, 1)
        mid[pl.ds(ih, PAIRS, stride=8), :] = line
    everything = mid[...]
    packed[...] = everything.reshape(PAIRS, 8, 128).astype(jnp.bfloat16)
    for b in range(2):
        halves = []
        for half in range(2):
            by = 64 * b + 32 * half
            turned_b = pltpu.roll(everything, 128 - by, 1) if by else everything
            halves.append(turned_b[:, :32].reshape(PAIRS, 8, 32))
        stored[:, b] = jnp.concatenate(halves, axis=1).astype(jnp.bfloat16)
    for halo in halos:
        halo.wait_send()


def front(raw):
    vm = pl.BlockSpec(memory_space=pltpu.VMEM)
    anywhere = pl.BlockSpec(memory_space=pl.ANY)
    dma = pltpu.SemaphoreType.DMA
    bf16, f32 = jnp.bfloat16, jnp.float32
    return pl.pallas_call(
        front_kernel,
        out_shape=(
            jax.ShapeDtypeStruct((PAIRS, 2, CD, 32), bf16),
            jax.ShapeDtypeStruct((PAIRS, 8, 128), bf16),
        ),
        in_specs=[anywhere] * 5,
        out_specs=(vm, vm),
        scratch_shapes=[
            pltpu.VMEM(raw.shape, bf16),
            pltpu.VMEM((CD, LEAD), bf16),
            pltpu.VMEM((CD, TAIL), bf16),
            pltpu.VMEM((2, 2 * F, KP), bf16),
            pltpu.VMEM((F, F), f32),
            pltpu.VMEM((768, 256), bf16),
            pltpu.VMEM((256, 256), bf16),
            pltpu.VMEM((NBLK + 2, CD, 256), bf16),
            pltpu.VMEM((CD, 17280), f32),
            pltpu.VMEM((CD * (WD + 1), KP), bf16),
            pltpu.VMEM((512, 128), f32),
            dma((5,)),
            dma((2,)),
            dma((2,)),
        ],
        compiler_params=pltpu.CompilerParams(
            vmem_limit_bytes=60 * 1024 * 1024, collective_id=1, has_side_effects=True
        ),
        name="front",
    )(raw, build_table(), build_kernel(), build_band(), build_swap())


def cross_kernel(packed, out, land, flat, both, left, result, own_sem, s1, r1, sy, ry, sp, rp, so, ro):
    t = lax.axis_index("tm")
    c = lax.axis_index("chan")
    h, x, k = c // 8, (c // 2) % 4, c % 2

    def chan(dh, dx):
        return ((h + dh) % 4) * 8 + ((x + dx) % 4) * 2 + k

    partner = c + 1 - 2 * k
    others = [(dt, dx) for dx in range(4) for dt in range(16) if dt or dx]
    barrier = pltpu.get_barrier_semaphore()
    for dt, dx in others:
        pl.semaphore_signal(
            barrier, inc=1, device_id=((t + dt) % 16, chan(0, dx)), device_id_type=MESH
        )
    for other in (chan(1, 0), chan(3, 0), partner):
        pl.semaphore_signal(barrier, inc=1, device_id=(t, other), device_id_type=MESH)
    pl.semaphore_wait(barrier, len(others) + 3)

    place = land.at[t % 2, x, t // 2]
    own = pltpu.make_async_copy(packed.at[t, x], place, own_sem)
    own.start()
    for dt, dx in others:
        to_t, to_x = (t + dt) % 16, (x + dx) % 4
        pltpu.make_async_remote_copy(
            src_ref=packed.at[to_t, to_x],
            dst_ref=place,
            send_sem=s1,
            recv_sem=r1,
            device_id=(to_t, chan(0, dx)),
            device_id_type=MESH,
        ).start()
    own.wait()
    count = flat.at[pl.ds(0, len(others))]
    pltpu.make_async_copy(count, count, r1).wait()

    lane = lax.broadcasted_iota(jnp.int32, (256, 128), 1)
    low = (lane // 32) % 2 == 0
    even = land[0].astype(jnp.float32).reshape(256, 128)
    odd = land[1].astype(jnp.float32).reshape(256, 128)
    half0 = jnp.where(low, even, pltpu.roll(odd, 32, 1)).reshape(4, 8, 8, 128)
    half1 = jnp.where(low, pltpu.roll(even, 96, 1), odd).reshape(4, 8, 8, 128)
    lane = lax.broadcasted_iota(jnp.int32, (CD, 128), 1)
    real = (lane // 16) % 2 == 0
    tiles = {}
    for i in range(4):
        for p in range(8):
            tile = jnp.concatenate([half0[i, p], half1[i, p]], axis=0)
            both[h, i, k, :, 128 * p : 128 * p + 128] = tile.astype(jnp.bfloat16)
            tiles[i, p] = tile

    pending = []

    def send(src, dst, to, send_sem, recv_sem):
        copy = pltpu.make_async_remote_copy(
            src_ref=src,
            dst_ref=dst,
            send_sem=send_sem,
            recv_sem=recv_sem,
            device_id=(t, to),
            device_id_type=MESH,
        )
        copy.start()
        pending.append(copy)

    def landed(ref, sem):
        pltpu.make_async_copy(ref, ref, sem).wait()

    def piece(dh, a, core):
        return both.at[(h + dh) % 4, pl.ds(2 * a, 2), core]

    def along_y(dh, a, by, send_sem):
        seen_as = (dh - by) % 4
        ref = piece(dh, a, k)
        send(ref, ref, chan(by, 0), send_sem, ry.at[seen_as - 1, a])

    def to_partner(dh, a):
        ref = piece(dh, a, k)
        send(ref, ref, partner, sp.at[dh, a], rp.at[dh, a])

    along_y(0, 0, 1, sy.at[0, 0])
    along_y(0, 1, 3, sy.at[1, 1])
    to_partner(0, 0)
    to_partner(0, 1)
    along_y(0, 1, 1, sy.at[0, 1])
    along_y(0, 0, 3, sy.at[1, 0])

    for (i, p), tile in tiles.items():
        flipped = jnp.where(real, pltpu.roll(tile, 112, 1), -pltpu.roll(tile, 16, 1))
        for r, source in enumerate((tile, flipped)):
            for b in range(2):
                kept = jnp.where(lane // 64 == b, source, 0.0).astype(jnp.bfloat16)
                left[r, b, i, :, 128 * p : 128 * p + 128] = kept

    def columns(dh):
        return pl.ds(pl.multiple_of(((h + dh) % 4) * 128, 128), 128)

    def compute(dh):
        for a in range(2):
            landed(piece(dh, a, 1 - k), rp.at[dh, a])
        part = lax.dot_general(
            left[...].reshape(256, 1024),
            both[(h + dh) % 4].reshape(128, 1024),
            (((1,), (1,)), ((), ())),
            preferred_element_type=jnp.float32,
        )
        result[dh] = part.reshape(2, 2, 4, CD, 128)
        bins = pl.ds(2 * x, 2)
        for e in (2, 1, 3):
            send(
                result.at[dh, :, :, (x + e) % 4],
                out.at[:, bins, :, columns(dh)],
                chan(0, e),
                so.at[dh, e],
                ro.at[dh, e],
            )
        stay = pltpu.make_async_copy(
            result.at[dh, :, :, x], out.at[:, bins, :, columns(dh)], so.at[dh, 0]
        )
        stay.start()
        return stay

    stays = [compute(0)]
    landed(piece(3, 0, k), ry.at[2, 0])
    along_y(3, 0, 1, sy.at[2, 0])
    to_partner(3, 0)
    landed(piece(1, 1, k), ry.at[0, 1])
    along_y(1, 1, 3, sy.at[2, 1])
    to_partner(1, 1)
    landed(piece(3, 1, k), ry.at[2, 1])
    to_partner(3, 1)
    landed(piece(1, 0, k), ry.at[0, 0])
    to_partner(1, 0)
    stays.append(compute(3))
    stays.append(compute(1))
    landed(piece(2, 0, k), ry.at[1, 0])
    to_partner(2, 0)
    landed(piece(2, 1, k), ry.at[1, 1])
    to_partner(2, 1)
    stays.append(compute(2))
    for dh in (0, 3, 1, 2):
        for e in (1, 2, 3):
            landed(out.at[:, pl.ds(2 * ((x - e) % 4), 2), :, columns(dh)], ro.at[dh, e])
    for copy in pending:
        copy.wait_send()
    for stay in stays:
        stay.wait()
    pltpu.make_async_copy(count, count, s1).wait()


def cross(packed):
    dma = pltpu.SemaphoreType.DMA
    bf16, f32 = jnp.bfloat16, jnp.float32
    return pl.pallas_call(
        cross_kernel,
        out_shape=jax.ShapeDtypeStruct((2, 8, CD, 512), f32),
        in_specs=[pl.BlockSpec(memory_space=pltpu.VMEM)],
        out_specs=pl.BlockSpec(memory_space=pl.ANY),
        scratch_shapes=[
            pltpu.VMEM((2, 4, 8, 8, 128), bf16),
            pltpu.VMEM((PAIRS, 8, 128), bf16),
            pltpu.VMEM((4, 4, 2, CD, 1024), bf16),
            pltpu.VMEM((2, 2, 4, CD, 1024), bf16),
            pltpu.VMEM((4, 2, 2, 4, CD, 128), f32),
            dma(()),
            dma(()),
            dma(()),
            dma((3, 2)),
            dma((3, 2)),
            dma((4, 2)),
            dma((4, 2)),
            dma((4, 4)),
            dma((4, 4)),
        ],
        compiler_params=pltpu.CompilerParams(
            vmem_limit_bytes=40 * 1024 * 1024, collective_id=0, has_side_effects=True
        ),
        name="cross",
    )(packed)


def on_device(raw):
    stored, packed = front(raw)
    totals = cross(packed.reshape(16, 4, 8, 128))
    return stored.reshape(F, CD, 2 * WD), totals * jnp.float32(1.0 / (16 * WD))


def solution(mesh):
    return jax.shard_map(
        on_device,
        mesh=mesh,
        in_specs=(P("chan", "tm"),),
        out_specs=(P(None, "chan", "tm"), P(None, "tm", "chan", None)),
        check_vma=False,
    )
```

time: 146 us -> 53.8 us (0.37)
  waiting for transfers between devices: 58.6 us -> 0 us
  Pallas kernels: 0 us -> 50 us
  local copies, waits for them, and re-layouts: 22.8 us -> 2.13 us
  blocking collectives: 20.3 us -> 0 us
  other arithmetic: 18.1 us -> 0.84 us
  between operations: 14.3 us -> 0.65 us
  starting transfers between devices: 6.75 us -> 0 us
  matrix products: 4.31 us -> 0 us
    all_gather x1 -> x0, waiting for transfers between devices: 57.9 us -> none  [on_device(): everyone = lax.all_gather(owned, 'chan', axis=1, tiled=True)]
    pallas_call x0 -> x2, Pallas kernels: none -> 50 us  [the longest x1 33.7 us: cross(): pl.pallas_call(cross_kernel, out_shape=jax.ShapeDtypeStruct((2, 8, CD, 51...]
    all_to_all x1 -> x0, blocking collectives: 20.3 us -> none  [on_device(): lax.all_to_all(stored, 'tm', split_axis=0, concat_axis=2, tiled=True)]
    another operation x5 -> x0, other arithmetic: 14.5 us -> none
    ppermute x2 -> x0, starting transfers between devices: 6.71 us -> none  [from_behind(): return lax.ppermute(x, axis, pairs)]
    reshape x6 -> x0, local copies, waits for them, and re-layouts: 6.61 us -> none
    slice x7 -> x0, local copies, waits for them, and re-layouts: 4.6 us -> none  [the longest x1 1.93 us: on_device(): split_parts[:, :, :, 1]]
    another operation x6 -> x0, local copies, waits for them, and re-layouts: 3.98 us -> none
  transfers between devices with their start and end apart: 3 -> 0, of which waited for: 2 -> 0; matrix products, arithmetic and copies ran while one was open for 6% -> 0% of each run, Pallas kernels for 0% -> 0%
where the time goes in v3:
time: 53.8 us; the launch traced here: 53.6 us
  Pallas kernels  50 us (93%)
  local copies, waits for them, and re-layouts  2.13 us (4%)
  other arithmetic  0.84 us (2%)
  between operations  0.65 us (1%)
    pallas_call x1, Pallas kernels, cross(): pl.pallas_call(cross_kernel, out_shape=jax.ShapeDtypeStruct((2, 8, CD, 51...  33.7 us
    pallas_call x1, Pallas kernels, front(): pl.pallas_call(front_kernel, out_shape=(jax.ShapeDtypeStruct((PAIRS, 2, C...  16.3 us
    unnamed x3, local copies, waits for them, and re-layouts  2.13 us

profile of v3, /device:TPU:1, one launch (start us, length us, event | category | flops | bytes accessed | tf_op | source)
XLA Modules:
  0.0 53.6 jit_solution(6629639597316226617)
XLA Ops:
  0.6 16.3 %front.1 = (bf16[64,2,16,32]{3,2,1,0:T(8,128)(2,1)}, bf16[64,8,128]{2,1,0:T(8,128)(2,1)}) custom-call(bf16[16,16000]{1,0:T(8,128)(2,1)} %raw_hbm.1, bf16[2,256,1024]{2,1,0:T(8,128)(2,1)} %constant.10.clone.table_hbm, f32[128,128]{1,0:T(8,128)} %constant.11.clone.kern_hbm, bf16[768,256]{1,0:T(8,128)(2,1)} %constant.12.clone.band_hbm, ...), custom_call_target="tpu_custom_call" | custom-call | tf_op jit(solution)/shard_map/front/pallas_call | solution.py:183
  16.9 0.0 copy-start
  16.9 2.1 %copy.7 = bf16[128,16,32]{0,2,1:T(8,128)(2,1)} copy(bf16[128,16,32]{2,1,0:T(8,128)(2,1)} %bitcast.3) | data formatting | bytes 262144
  19.1 0.0 copy-done
  19.1 33.7 %cross.1 = f32[2,8,16,512]{3,2,1,0:T(8,128)S(1)} custom-call(bf16[16,4,8,128]{3,2,1,0:T(8,128)(2,1)S(1)} %bitcast.2), custom_call_target="tpu_custom_call" | custom-call | tf_op jit(solution)/shard_map/cross/pallas_call | solution.py:367
  52.8 0.8 %broadcast_multiply_fusion = f32[2,8,16,512]{3,2,1,0:T(8,128)} fusion(f32[2,8,16,512]{3,2,1,0:T(8,128)S(1)} %cross.1), kind=kLoop, calls=%fused_computation | loop fusion | flops 131072 | bytes 1048576 | tf_op jit(solution)/shard_map/mul | solution.py:398
Async XLA Ops:
  16.9 2.1 %copy-start = (bf16[64,8,128]{2,1,0:T(8,128)(2,1)S(1)}, bf16[64,8,128]{2,1,0:T(8,128)(2,1)}, u32[]{:S(2)}) copy-start(bf16[64,8,128]{2,1,0:T(8,128)(2,1)} %get-tuple-element.5) | copy-start | bytes 393220

commit v4 on v3

--- a/solution.py
+++ b/solution.py
@@ -64,19 +64,9 @@
     return jnp.asarray(out.astype(jnp.bfloat16))
 
 
-def front_kernel(
-    raw_hbm, table_hbm, kern_hbm, band_hbm, swap_hbm, stored, packed,
-    raw, lead, tail, table, kern, band, swap, ext, norm, pieces, mid, load_sem, halo_send, halo_recv
-):
+def halo_kernel(raw, lead, tail, send_sem, recv_sem):
     t = lax.axis_index("tm")
     c = lax.axis_index("chan")
-    loads = []
-    for n, (src, dst) in enumerate(
-        ((raw_hbm, raw), (band_hbm, band), (table_hbm, table), (kern_hbm, kern), (swap_hbm, swap))
-    ):
-        load = pltpu.make_async_copy(src, dst, load_sem.at[n])
-        load.start()
-        loads.append(load)
     after, before = (t + 1) % 16, (t + 15) % 16
     barrier = pltpu.get_barrier_semaphore()
     for other in (after, before):
@@ -84,25 +74,53 @@
     pl.semaphore_wait(barrier, 2)
     halos = []
     for n, (first, count, dst, other) in enumerate(
-        ((raw_hbm.shape[1] - LEAD, LEAD, lead, after), (0, TAIL, tail, before))
+        ((raw.shape[1] - LEAD, LEAD, lead, after), (0, TAIL, tail, before))
     ):
         halo = pltpu.make_async_remote_copy(
-            src_ref=raw_hbm.at[:, first : first + count],
+            src_ref=raw.at[:, first : first + count],
             dst_ref=dst,
-            send_sem=halo_send.at[n],
-            recv_sem=halo_recv.at[n],
+            send_sem=send_sem.at[n],
+            recv_sem=recv_sem.at[n],
             device_id=(other, c),
             device_id_type=MESH,
         )
         halo.start()
         halos.append(halo)
-    loads[0].wait()
+    for halo in halos:
+        halo.wait()
+
+
+def exchange_rims(raw):
+    anywhere = pl.BlockSpec(memory_space=pl.ANY)
+    dma = pltpu.SemaphoreType.DMA
+    return pl.pallas_call(
+        halo_kernel,
+        out_shape=(
+            jax.ShapeDtypeStruct((CD, LEAD), raw.dtype),
+            jax.ShapeDtypeStruct((CD, TAIL), raw.dtype),
+        ),
+        in_specs=[anywhere],
+        out_specs=(anywhere, anywhere),
+        scratch_shapes=[dma((2,)), dma((2,))],
+        compiler_params=pltpu.CompilerParams(collective_id=1, has_side_effects=True),
+        name="rims",
+    )(raw)
+
+
+def front_part(
+    t, hbm, raw, lead, tail, table, kern, band, swap, ext, norm, pieces, mid, packed, load_sem
+):
+    loads = []
+    for n, (src, dst) in enumerate(zip(hbm, (raw, lead, tail, band, table, kern, swap))):
+        load = pltpu.make_async_copy(src, dst, load_sem.at[n])
+        load.start()
+        loads.append(load)
+    for load in loads[:3]:
+        load.wait()
     for i in range(62):
         ext[1 + i] = raw[:, 256 * i : 256 * i + 256]
     ext[63, :, 0:128] = raw[:, 15872:16000]
     ext[68, :, 128:256] = jnp.zeros((CD, 128), jnp.bfloat16)
-    for halo in halos:
-        halo.wait_recv()
     has_lead = jnp.full((CD, LEAD), t, jnp.int32) > 0
     has_tail = jnp.full((CD, TAIL), t, jnp.int32) < 15
     ext[0] = jnp.where(has_lead, lead[...].astype(jnp.float32), 0.0).astype(jnp.bfloat16)
@@ -111,7 +129,7 @@
     for j in range(4):
         ext[64 + j] = behind[:, 128 + 256 * j : 384 + 256 * j]
     ext[68, :, 0:128] = behind[:, 1152:1280]
-    for load in loads[1:]:
+    for load in loads[3:]:
         load.wait()
 
     box = jnp.zeros((NBLK * CD, 256), jnp.float32)
@@ -163,55 +181,29 @@
             line = pltpu.roll(line, 128 - 16 * ih, 1)
         mid[pl.ds(ih, PAIRS, stride=8), :] = line
     everything = mid[...]
-    packed[...] = everything.reshape(PAIRS, 8, 128).astype(jnp.bfloat16)
-    for b in range(2):
-        halves = []
-        for half in range(2):
-            by = 64 * b + 32 * half
-            turned_b = pltpu.roll(everything, 128 - by, 1) if by else everything
-            halves.append(turned_b[:, :32].reshape(PAIRS, 8, 32))
-        stored[:, b] = jnp.concatenate(halves, axis=1).astype(jnp.bfloat16)
-    for halo in halos:
-        halo.wait_send()
-
-
-def front(raw):
-    vm = pl.BlockSpec(memory_space=pltpu.VMEM)
-    anywhere = pl.BlockSpec(memory_space=pl.ANY)
-    dma = pltpu.SemaphoreType.DMA
-    bf16, f32 = jnp.bfloat16, jnp.float32
-    return pl.pallas_call(
-        front_kernel,
-        out_shape=(
-            jax.ShapeDtypeStruct((PAIRS, 2, CD, 32), bf16),
-            jax.ShapeDtypeStruct((PAIRS, 8, 128), bf16),
-        ),
-        in_specs=[anywhere] * 5,
-        out_specs=(vm, vm),
-        scratch_shapes=[
-            pltpu.VMEM(raw.shape, bf16),
-            pltpu.VMEM((CD, LEAD), bf16),
-            pltpu.VMEM((CD, TAIL), bf16),
-            pltpu.VMEM((2, 2 * F, KP), bf16),
-            pltpu.VMEM((F, F), f32),
-            pltpu.VMEM((768, 256), bf16),
-            pltpu.VMEM((256, 256), bf16),
-            pltpu.VMEM((NBLK + 2, CD, 256), bf16),
-            pltpu.VMEM((CD, 17280), f32),
-            pltpu.VMEM((CD * (WD + 1), KP), bf16),
-            pltpu.VMEM((512, 128), f32),
-            dma((5,)),
-            dma((2,)),
-            dma((2,)),
-        ],
-        compiler_params=pltpu.CompilerParams(
-            vmem_limit_bytes=60 * 1024 * 1024, collective_id=1, has_side_effects=True
-        ),
-        name="front",
-    )(raw, build_table(), build_kernel(), build_band(), build_swap())
-
-
-def cross_kernel(packed, out, land, flat, both, left, result, own_sem, s1, r1, sy, ry, sp, rp, so, ro):
+    packed[...] = everything.reshape(16, 4, 8, 128).astype(jnp.bfloat16)
+    return white
+
+def store_part(white, swap, stored):
+    row = lax.broadcasted_iota(jnp.int32, (F, F), 0)
+    column = lax.broadcasted_iota(jnp.int32, (F, F), 1)
+    order = jnp.where(column == 2 * (row % PAIRS) + row // PAIRS, 1.0, 0.0).astype(jnp.bfloat16)
+    for r in range(2):
+        turned = lax.dot_general(
+            swap[...],
+            white[r * F : r * F + F],
+            (((1,), (1,)), ((), ())),
+            preferred_element_type=jnp.float32,
+        ).astype(jnp.bfloat16)
+        turned = jnp.dot(turned, order, preferred_element_type=jnp.float32)
+        stored[:, r * WD : r * WD + WD, :] = turned.reshape(CD, WD, F).astype(jnp.bfloat16)
+
+
+def main_kernel(
+    raw_hbm, lead_hbm, tail_hbm, band_hbm, table_hbm, kern_hbm, swap_hbm, stored, out,
+    raw, lead, tail, table, kern, band, swap, ext, norm, pieces, mid, packed,
+    land, flat, both, left, result, load_sem, own_sem, s1, r1, sy, ry, sp, rp, so, ro
+):
     t = lax.axis_index("tm")
     c = lax.axis_index("chan")
     h, x, k = c // 8, (c // 2) % 4, c % 2
@@ -228,6 +220,10 @@
         )
     for other in (chan(1, 0), chan(3, 0), partner):
         pl.semaphore_signal(barrier, inc=1, device_id=(t, other), device_id_type=MESH)
+    hbm = (raw_hbm, lead_hbm, tail_hbm, band_hbm, table_hbm, kern_hbm, swap_hbm)
+    white = front_part(
+        t, hbm, raw, lead, tail, table, kern, band, swap, ext, norm, pieces, mid, packed, load_sem
+    )
     pl.semaphore_wait(barrier, len(others) + 3)
 
     place = land.at[t % 2, x, t // 2]
@@ -244,6 +240,7 @@
             device_id_type=MESH,
         ).start()
     own.wait()
+    store_part(white, swap, stored)
     count = flat.at[pl.ds(0, len(others))]
     pltpu.make_async_copy(count, count, r1).wait()
 
@@ -280,7 +277,7 @@
         pltpu.make_async_copy(ref, ref, sem).wait()
 
     def piece(dh, a, core):
-        return both.at[(h + dh) % 4, pl.ds(2 * a, 2), core]
+        return both.at[(h + dh) % 4, pl.ds(1 * a, 1), core]
 
     def along_y(dh, a, by, send_sem):
         seen_as = (dh - by) % 4
@@ -292,11 +289,17 @@
         send(ref, ref, partner, sp.at[dh, a], rp.at[dh, a])
 
     along_y(0, 0, 1, sy.at[0, 0])
+    along_y(0, 2, 3, sy.at[1, 2])
+    to_partner(0, 0)
+    along_y(0, 1, 1, sy.at[0, 1])
+    along_y(0, 3, 3, sy.at[1, 3])
+    to_partner(0, 1)
+    along_y(0, 2, 1, sy.at[0, 2])
+    along_y(0, 0, 3, sy.at[1, 0])
+    to_partner(0, 2)
+    along_y(0, 3, 1, sy.at[0, 3])
     along_y(0, 1, 3, sy.at[1, 1])
-    to_partner(0, 0)
-    to_partner(0, 1)
-    along_y(0, 1, 1, sy.at[0, 1])
-    along_y(0, 0, 3, sy.at[1, 0])
+    to_partner(0, 3)
 
     for (i, p), tile in tiles.items():
         flipped = jnp.where(real, pltpu.roll(tile, 112, 1), -pltpu.roll(tile, 16, 1))
@@ -309,7 +312,7 @@
         return pl.ds(pl.multiple_of(((h + dh) % 4) * 128, 128), 128)
 
     def compute(dh):
-        for a in range(2):
+        for a in range(4):
             landed(piece(dh, a, 1 - k), rp.at[dh, a])
         part = lax.dot_general(
             left[...].reshape(256, 1024),
@@ -337,19 +340,33 @@
     landed(piece(3, 0, k), ry.at[2, 0])
     along_y(3, 0, 1, sy.at[2, 0])
     to_partner(3, 0)
-    landed(piece(1, 1, k), ry.at[0, 1])
-    along_y(1, 1, 3, sy.at[2, 1])
-    to_partner(1, 1)
+    landed(piece(1, 2, k), ry.at[0, 2])
+    along_y(1, 2, 3, sy.at[2, 2])
+    to_partner(1, 2)
     landed(piece(3, 1, k), ry.at[2, 1])
+    along_y(3, 1, 1, sy.at[2, 1])
     to_partner(3, 1)
+    landed(piece(1, 3, k), ry.at[0, 3])
+    along_y(1, 3, 3, sy.at[2, 3])
+    to_partner(1, 3)
+    landed(piece(3, 2, k), ry.at[2, 2])
+    to_partner(3, 2)
     landed(piece(1, 0, k), ry.at[0, 0])
     to_partner(1, 0)
+    landed(piece(3, 3, k), ry.at[2, 3])
+    to_partner(3, 3)
+    landed(piece(1, 1, k), ry.at[0, 1])
+    to_partner(1, 1)
     stays.append(compute(3))
     stays.append(compute(1))
     landed(piece(2, 0, k), ry.at[1, 0])
     to_partner(2, 0)
+    landed(piece(2, 2, k), ry.at[1, 2])
+    to_partner(2, 2)
     landed(piece(2, 1, k), ry.at[1, 1])
     to_partner(2, 1)
+    landed(piece(2, 3, k), ry.at[1, 3])
+    to_partner(2, 3)
     stays.append(compute(2))
     for dh in (0, 3, 1, 2):
         for e in (1, 2, 3):
@@ -361,41 +378,58 @@
     pltpu.make_async_copy(count, count, s1).wait()
 
 
-def cross(packed):
+def main(raw, lead, tail):
+    vm = pl.BlockSpec(memory_space=pltpu.VMEM)
+    anywhere = pl.BlockSpec(memory_space=pl.ANY)
     dma = pltpu.SemaphoreType.DMA
     bf16, f32 = jnp.bfloat16, jnp.float32
     return pl.pallas_call(
-        cross_kernel,
-        out_shape=jax.ShapeDtypeStruct((2, 8, CD, 512), f32),
-        in_specs=[pl.BlockSpec(memory_space=pltpu.VMEM)],
-        out_specs=pl.BlockSpec(memory_space=pl.ANY),
+        main_kernel,
+        out_shape=(
+            jax.ShapeDtypeStruct((CD, 2 * WD, F), bf16),
+            jax.ShapeDtypeStruct((2, 8, CD, 512), f32),
+        ),
+        in_specs=[anywhere] * 7,
+        out_specs=(vm, anywhere),
         scratch_shapes=[
+            pltpu.VMEM(raw.shape, bf16),
+            pltpu.VMEM((CD, LEAD), bf16),
+            pltpu.VMEM((CD, TAIL), bf16),
+            pltpu.VMEM((2, 2 * F, KP), bf16),
+            pltpu.VMEM((F, F), f32),
+            pltpu.VMEM((768, 256), bf16),
+            pltpu.VMEM((256, 256), bf16),
+            pltpu.VMEM((NBLK + 2, CD, 256), bf16),
+            pltpu.VMEM((CD, 17280), f32),
+            pltpu.VMEM((CD * (WD + 1), KP), bf16),
+            pltpu.VMEM((512, 128), f32),
+            pltpu.VMEM((16, 4, 8, 128), bf16),
             pltpu.VMEM((2, 4, 8, 8, 128), bf16),
             pltpu.VMEM((PAIRS, 8, 128), bf16),
             pltpu.VMEM((4, 4, 2, CD, 1024), bf16),
             pltpu.VMEM((2, 2, 4, CD, 1024), bf16),
             pltpu.VMEM((4, 2, 2, 4, CD, 128), f32),
+            dma((7,)),
             dma(()),
             dma(()),
             dma(()),
-            dma((3, 2)),
-            dma((3, 2)),
-            dma((4, 2)),
-            dma((4, 2)),
+            dma((3, 4)),
+            dma((3, 4)),
+            dma((4, 4)),
+            dma((4, 4)),
             dma((4, 4)),
             dma((4, 4)),
         ],
         compiler_params=pltpu.CompilerParams(
-            vmem_limit_bytes=40 * 1024 * 1024, collective_id=0, has_side_effects=True
+            vmem_limit_bytes=58 * 1024 * 1024, collective_id=0, has_side_effects=True
         ),
-        name="cross",
-    )(packed)
+        name="main",
+    )(raw, lead, tail, build_band(), build_table(), build_kernel(), build_swap())
 
 
 def on_device(raw):
-    stored, packed = front(raw)
-    totals = cross(packed.reshape(16, 4, 8, 128))
-    return stored.reshape(F, CD, 2 * WD), totals * jnp.float32(1.0 / (16 * WD))
+    stored, totals = main(raw, *exchange_rims(raw))
+    return jnp.transpose(stored, (2, 0, 1)), totals * jnp.float32(1.0 / (16 * WD))
 
 
 def solution(mesh):

time: 53.8 us -> 50.6 us (0.941)
  Pallas kernels: 50 us -> 47.1 us
  local copies, waits for them, and re-layouts: 2.13 us -> 0.66 us
  other arithmetic: 0.84 us -> 1.92 us
    pallas_call x2, Pallas kernels: 50 us -> 47.1 us  [the longest x1 34.2 us: main(): pl.pallas_call(main_kernel, out_shape=(jax.ShapeDtypeStruct((CD, 2 * WD,...]
    unnamed x3, local copies, waits for them, and re-layouts: 2.13 us -> 0.66 us
    mul x1, other arithmetic: 0.84 us -> 1.92 us  [on_device(): totals * jnp.float32(1.0 / (16 * WD))]
where the time goes in v4:
time: 50.6 us; the launch traced here: 50.4 us
  Pallas kernels  47.1 us (93%)
  other arithmetic  1.92 us (4%)
  local copies, waits for them, and re-layouts  0.66 us (1%)
  between operations  0.65 us (1%)
    pallas_call x1, Pallas kernels, main(): pl.pallas_call(main_kernel, out_shape=(jax.ShapeDtypeStruct((CD, 2 * WD,...  34.2 us
    pallas_call x1, Pallas kernels, exchange_rims(): pl.pallas_call(halo_kernel, out_shape=(jax.ShapeDtypeStruct((CD, LEAD), r...  13 us
    mul x1, other arithmetic, on_device(): totals * jnp.float32(1.0 / (16 * WD))  1.92 us

profile of v4, /device:TPU:1, one launch (start us, length us, event | category | flops | bytes accessed | tf_op | source)
XLA Modules:
  0.0 50.4 jit_solution(10027312883977991396)
XLA Ops:
  0.6 13.0 %rims.1 = (bf16[16,256]{1,0:T(8,128)(2,1)}, bf16[16,1280]{1,0:T(8,128)(2,1)}) custom-call(bf16[16,16000]{1,0:T(8,128)(2,1)} %raw_hbm.1), custom_call_target="tpu_custom_call" | custom-call | tf_op jit(solution)/shard_map/rims/pallas_call | solution.py:96
  13.6 34.2 %main.1 = (bf16[16,32,128]{2,1,0:T(8,128)(2,1)}, f32[2,8,16,512]{3,2,1,0:T(8,128)}) custom-call(bf16[16,16000]{1,0:T(8,128)(2,1)} %raw_hbm.1, bf16[16,256]{1,0:T(8,128)(2,1)} %get-tuple-element.6.lead_hbm, bf16[16,1280]{1,0:T(8,128)(2,1)} %get-tuple-element.7.tail_hbm, bf16[768,256]{1,0:T(8,128)(2,1)} %constant.10.clone.band_hbm, ...), custom_call_target="tpu_custom_call" | custom-call | tf_op jit(solution)/shard_map/main/pallas_call | solution.py:386
  47.8 0.0 copy-start
  47.8 1.9 %broadcast_multiply_fusion = f32[2,8,16,512]{3,2,1,0:T(8,128)} fusion(f32[2,8,16,512]{3,2,1,0:T(8,128)} %get-tuple-element.9), kind=kLoop, calls=%fused_computation | loop fusion | flops 131072 | bytes 1048576 | tf_op jit(solution)/shard_map/mul | solution.py:432
  49.7 0.0 copy-done
  49.7 0.7 %copy.8 = bf16[128,16,32]{0,2,1:T(8,128)(2,1)} copy(bf16[128,16,32]{0,2,1:T(8,128)(2,1)S(1)} %bitcast.1) | data formatting | bytes 262144
Async XLA Ops:
  47.8 1.9 %copy-start = (bf16[16,32,128]{2,1,0:T(8,128)(2,1)S(1)}, bf16[16,32,128]{2,1,0:T(8,128)(2,1)}, u32[]{:S(2)}) copy-start(bf16[16,32,128]{2,1,0:T(8,128)(2,1)} %get-tuple-element.8) | copy-start | bytes 393220

commit v5 on v4

--- a/solution.py
+++ b/solution.py
@@ -39,32 +39,7 @@
     return jnp.asarray(out.astype(jnp.bfloat16))
 
 
-def build_kernel():
-    positions = np.arange(F, dtype=np.float32)
-    distance = positions[:, None] - positions[None, :]
-    weights = np.exp(-distance * distance / np.float32(2.0 * SMOOTH * SMOOTH))
-    weights = weights / np.sum(weights, axis=1, keepdims=True, dtype=np.float32)
-    order = bin_order()
-    return jnp.asarray(weights[order][:, order].astype(np.float32))
-
-
-def build_band():
-    i = np.arange(3 * 256)[:, None]
-    j = np.arange(256)[None, :]
-    first = LEAD - RM
-    band = (i - j >= first) & (i - j <= first + 2 * RM)
-    return jnp.asarray(band.astype(np.float32).astype(jnp.bfloat16))
-
-
-def build_swap():
-    out = np.zeros((256, 256), np.float32)
-    for w in range(WD):
-        for c in range(CD):
-            out[w * CD + c, c * WD + w] = 1.0
-    return jnp.asarray(out.astype(jnp.bfloat16))
-
-
-def halo_kernel(raw, lead, tail, send_sem, recv_sem):
+def halo_kernel(raw, rims, send_sem, recv_sem):
     t = lax.axis_index("tm")
     c = lax.axis_index("chan")
     after, before = (t + 1) % 16, (t + 15) % 16
@@ -74,11 +49,11 @@
     pl.semaphore_wait(barrier, 2)
     halos = []
     for n, (first, count, dst, other) in enumerate(
-        ((raw.shape[1] - LEAD, LEAD, lead, after), (0, TAIL, tail, before))
+        ((raw.shape[1] - LEAD, LEAD, 0, after), (0, TAIL, LEAD, before))
     ):
         halo = pltpu.make_async_remote_copy(
             src_ref=raw.at[:, first : first + count],
-            dst_ref=dst,
+            dst_ref=rims.at[:, dst : dst + count],
             send_sem=send_sem.at[n],
             recv_sem=recv_sem.at[n],
             device_id=(other, c),
@@ -95,27 +70,40 @@
     dma = pltpu.SemaphoreType.DMA
     return pl.pallas_call(
         halo_kernel,
-        out_shape=(
-            jax.ShapeDtypeStruct((CD, LEAD), raw.dtype),
-            jax.ShapeDtypeStruct((CD, TAIL), raw.dtype),
+        out_shape=jax.ShapeDtypeStruct((CD, LEAD + TAIL), raw.dtype),
+        in_specs=[anywhere],
+        out_specs=anywhere,
+        scratch_shapes=[dma((2,)), dma((2,))],
+        compiler_params=pltpu.CompilerParams(
+            vmem_limit_bytes=54784 * 1024, collective_id=1, has_side_effects=True
         ),
-        in_specs=[anywhere],
-        out_specs=(anywhere, anywhere),
-        scratch_shapes=[dma((2,)), dma((2,))],
-        compiler_params=pltpu.CompilerParams(collective_id=1, has_side_effects=True),
         name="rims",
     )(raw)
 
 
 def front_part(
-    t, hbm, raw, lead, tail, table, kern, band, swap, ext, norm, pieces, mid, packed, load_sem
+    t, hbm, raw, rims, table, kern, band, swap, ext, norm, pieces, mid, packed, load_sem
 ):
     loads = []
-    for n, (src, dst) in enumerate(zip(hbm, (raw, lead, tail, band, table, kern, swap))):
+    for n, (src, dst) in enumerate(zip(hbm, (raw, rims, table))):
         load = pltpu.make_async_copy(src, dst, load_sem.at[n])
         load.start()
         loads.append(load)
-    for load in loads[:3]:
+    row = lax.broadcasted_iota(jnp.int32, (F, F), 0)
+    column = lax.broadcasted_iota(jnp.int32, (F, F), 1)
+    apart = 2 * (row % PAIRS) + row // PAIRS - 2 * (column % PAIRS) - column // PAIRS
+    apart = apart.astype(jnp.float32)
+    weights = jnp.exp(-apart * apart / jnp.float32(2.0 * SMOOTH * SMOOTH))
+    kern[...] = weights / jnp.sum(weights, axis=1, keepdims=True)
+    row = lax.broadcasted_iota(jnp.int32, (256, 256), 0)
+    column = lax.broadcasted_iota(jnp.int32, (256, 256), 1)
+    turn = column == row % CD * WD + row // CD
+    swap[...] = jnp.where(turn, 1.0, 0.0).astype(jnp.bfloat16)
+    row = lax.broadcasted_iota(jnp.int32, (3 * 256, 256), 0)
+    column = lax.broadcasted_iota(jnp.int32, (3 * 256, 256), 1)
+    inside = jnp.abs(row - column - LEAD) <= RM
+    band[...] = jnp.where(inside, 1.0, 0.0).astype(jnp.bfloat16)
+    for load in loads[:2]:
         load.wait()
     for i in range(62):
         ext[1 + i] = raw[:, 256 * i : 256 * i + 256]
@@ -123,13 +111,13 @@
     ext[68, :, 128:256] = jnp.zeros((CD, 128), jnp.bfloat16)
     has_lead = jnp.full((CD, LEAD), t, jnp.int32) > 0
     has_tail = jnp.full((CD, TAIL), t, jnp.int32) < 15
-    ext[0] = jnp.where(has_lead, lead[...].astype(jnp.float32), 0.0).astype(jnp.bfloat16)
-    behind = jnp.where(has_tail, tail[...].astype(jnp.float32), 0.0).astype(jnp.bfloat16)
+    ext[0] = jnp.where(has_lead, rims[:, :LEAD].astype(jnp.float32), 0.0).astype(jnp.bfloat16)
+    behind = jnp.where(has_tail, rims[:, LEAD:].astype(jnp.float32), 0.0).astype(jnp.bfloat16)
     ext[63, :, 128:256] = behind[:, 0:128]
     for j in range(4):
         ext[64 + j] = behind[:, 128 + 256 * j : 384 + 256 * j]
     ext[68, :, 0:128] = behind[:, 1152:1280]
-    for load in loads[3:]:
+    for load in loads[2:]:
         load.wait()
 
     box = jnp.zeros((NBLK * CD, 256), jnp.float32)
@@ -200,8 +188,8 @@
 
 
 def main_kernel(
-    raw_hbm, lead_hbm, tail_hbm, band_hbm, table_hbm, kern_hbm, swap_hbm, stored, out,
-    raw, lead, tail, table, kern, band, swap, ext, norm, pieces, mid, packed,
+    raw_hbm, rims_hbm, table_hbm, stored, out,
+    raw, rims, table, kern, band, swap, ext, norm, pieces, mid, packed,
     land, flat, both, left, result, load_sem, own_sem, s1, r1, sy, ry, sp, rp, so, ro
 ):
     t = lax.axis_index("tm")
@@ -213,6 +201,7 @@
 
     partner = c + 1 - 2 * k
     others = [(dt, dx) for dx in range(4) for dt in range(16) if dt or dx]
+    others.sort(key=lambda o: -min(o[0] % 8, 8 - o[0] % 8) - min(o[1], 4 - o[1]))
     barrier = pltpu.get_barrier_semaphore()
     for dt, dx in others:
         pl.semaphore_signal(
@@ -220,9 +209,9 @@
         )
     for other in (chan(1, 0), chan(3, 0), partner):
         pl.semaphore_signal(barrier, inc=1, device_id=(t, other), device_id_type=MESH)
-    hbm = (raw_hbm, lead_hbm, tail_hbm, band_hbm, table_hbm, kern_hbm, swap_hbm)
+    hbm = (raw_hbm, rims_hbm, table_hbm)
     white = front_part(
-        t, hbm, raw, lead, tail, table, kern, band, swap, ext, norm, pieces, mid, packed, load_sem
+        t, hbm, raw, rims, table, kern, band, swap, ext, norm, pieces, mid, packed, load_sem
     )
     pl.semaphore_wait(barrier, len(others) + 3)
 
@@ -336,13 +325,14 @@
         stay.start()
         return stay
 
-    stays = [compute(0)]
+    stays = []
     landed(piece(3, 0, k), ry.at[2, 0])
     along_y(3, 0, 1, sy.at[2, 0])
     to_partner(3, 0)
     landed(piece(1, 2, k), ry.at[0, 2])
     along_y(1, 2, 3, sy.at[2, 2])
     to_partner(1, 2)
+    stays.append(compute(0))
     landed(piece(3, 1, k), ry.at[2, 1])
     along_y(3, 1, 1, sy.at[2, 1])
     to_partner(3, 1)
@@ -378,7 +368,7 @@
     pltpu.make_async_copy(count, count, s1).wait()
 
 
-def main(raw, lead, tail):
+def main(raw, rims):
     vm = pl.BlockSpec(memory_space=pltpu.VMEM)
     anywhere = pl.BlockSpec(memory_space=pl.ANY)
     dma = pltpu.SemaphoreType.DMA
@@ -389,12 +379,11 @@
             jax.ShapeDtypeStruct((CD, 2 * WD, F), bf16),
             jax.ShapeDtypeStruct((2, 8, CD, 512), f32),
         ),
-        in_specs=[anywhere] * 7,
+        in_specs=[anywhere] * 3,
         out_specs=(vm, anywhere),
         scratch_shapes=[
             pltpu.VMEM(raw.shape, bf16),
-            pltpu.VMEM((CD, LEAD), bf16),
-            pltpu.VMEM((CD, TAIL), bf16),
+            pltpu.VMEM(rims.shape, bf16),
             pltpu.VMEM((2, 2 * F, KP), bf16),
             pltpu.VMEM((F, F), f32),
             pltpu.VMEM((768, 256), bf16),
@@ -409,7 +398,7 @@
             pltpu.VMEM((4, 4, 2, CD, 1024), bf16),
             pltpu.VMEM((2, 2, 4, CD, 1024), bf16),
             pltpu.VMEM((4, 2, 2, 4, CD, 128), f32),
-            dma((7,)),
+            dma((3,)),
             dma(()),
             dma(()),
             dma(()),
@@ -421,14 +410,14 @@
             dma((4, 4)),
         ],
         compiler_params=pltpu.CompilerParams(
-            vmem_limit_bytes=58 * 1024 * 1024, collective_id=0, has_side_effects=True
+            vmem_limit_bytes=53504 * 1024, collective_id=0, has_side_effects=True
         ),
         name="main",
-    )(raw, lead, tail, build_band(), build_table(), build_kernel(), build_swap())
+    )(raw, rims, build_table())
 
 
 def on_device(raw):
-    stored, totals = main(raw, *exchange_rims(raw))
+    stored, totals = main(raw, exchange_rims(raw))
     return jnp.transpose(stored, (2, 0, 1)), totals * jnp.float32(1.0 / (16 * WD))
 
 

time: 50.6 us -> 48.8 us (0.964)
  other arithmetic: 1.92 us -> 0.84 us
  Pallas kernels: 47.1 us -> 46.5 us
    mul x1, other arithmetic: 1.92 us -> 0.84 us  [on_device(): totals * jnp.float32(1.0 / (16 * WD))]
    pallas_call x1, Pallas kernels: 34.2 us -> 33.5 us  [main(): pl.pallas_call(main_kernel, out_shape=(jax.ShapeDtypeStruct((CD, 2 * WD,...]
where the time goes in v5:
time: 48.8 us; the launch traced here: 48.6 us
  Pallas kernels  46.5 us (95%)
  other arithmetic  0.84 us (2%)
  local copies, waits for them, and re-layouts  0.66 us (1%)
  between operations  0.66 us (1%)
    pallas_call x1, Pallas kernels, main(): pl.pallas_call(main_kernel, out_shape=(jax.ShapeDtypeStruct((CD, 2 * WD,...  33.5 us
    pallas_call x1, Pallas kernels, exchange_rims(): pl.pallas_call(halo_kernel, out_shape=jax.ShapeDtypeStruct((CD, LEAD + TA...  13 us

profile of v5, /device:TPU:1, one launch (start us, length us, event | category | flops | bytes accessed | tf_op | source)
XLA Modules:
  0.0 48.6 jit_solution(12331981588099279645)
XLA Ops:
  0.6 0.0 copy-start
  0.6 13.0 %rims.1.rims_hbm = bf16[16,1536]{1,0:T(8,128)(2,1)S(1)} custom-call(bf16[16,16000]{1,0:T(8,128)(2,1)} %raw_hbm.1), custom_call_target="tpu_custom_call" | custom-call | tf_op jit(solution)/shard_map/rims/pallas_call | solution.py:71
  13.6 0.0 copy-done
  13.6 33.5 %main.1 = (bf16[16,32,128]{2,1,0:T(8,128)(2,1)S(1)}, f32[2,8,16,512]{3,2,1,0:T(8,128)S(1)}) custom-call(bf16[16,16000]{1,0:T(8,128)(2,1)S(1)} %copy-done, bf16[16,1536]{1,0:T(8,128)(2,1)S(1)} %rims.1.rims_hbm, bf16[2,256,1024]{2,1,0:T(8,128)(2,1)} %constant.4.clone.table_hbm), custom_call_target="tpu_custom_call" | custom-call | tf_op jit(solution)/shard_map/main/pallas_call | solution.py:376
  47.1 0.8 %broadcast_multiply_fusion = f32[2,8,16,512]{3,2,1,0:T(8,128)} fusion(f32[2,8,16,512]{3,2,1,0:T(8,128)S(1)} %get-tuple-element.5), kind=kLoop, calls=%fused_computation | loop fusion | flops 131072 | bytes 1048576 | tf_op jit(solution)/shard_map/mul | solution.py:421
  48.0 0.7 %copy.5 = bf16[128,16,32]{0,2,1:T(8,128)(2,1)} copy(bf16[128,16,32]{0,2,1:T(8,128)(2,1)S(1)} %bitcast.1) | data formatting | bytes 262144
Async XLA Ops:
  0.6 13.0 %copy-start = (bf16[16,16000]{1,0:T(8,128)(2,1)S(1)}, bf16[16,16000]{1,0:T(8,128)(2,1)}, u32[]{:S(2)}) copy-start(bf16[16,16000]{1,0:T(8,128)(2,1)} %raw_hbm.1) | copy-start | bytes 1536004

commit v6 on v5

--- a/solution.py
+++ b/solution.py
@@ -117,9 +117,6 @@
     for j in range(4):
         ext[64 + j] = behind[:, 128 + 256 * j : 384 + 256 * j]
     ext[68, :, 0:128] = behind[:, 1152:1280]
-    for load in loads[2:]:
-        load.wait()
-
     box = jnp.zeros((NBLK * CD, 256), jnp.float32)
     for d in range(3):
         box += jnp.dot(
@@ -139,6 +136,8 @@
             wide = pltpu.roll(wide, 1152 - off, 1)
         pieces[CD * p : CD * p + CD, :] = wide[:, :KP].astype(jnp.bfloat16)
 
+    for load in loads[2:]:
+        load.wait()
     contract = (((1,), (1,)), ((), ()))
     spec = lax.dot_general(
         table[0], pieces[0 : WD * CD, :], contract, preferred_element_type=jnp.float32

time: 48.8 us -> 48.6 us (level)
  no operation moved by 1% of the time
where the time goes in v6:
time: 48.6 us; the launch traced here: 48.4 us
  Pallas kernels  46.3 us (95%)
  other arithmetic  0.84 us (2%)
  local copies, waits for them, and re-layouts  0.66 us (1%)
  between operations  0.66 us (1%)
    pallas_call x1, Pallas kernels, main(): pl.pallas_call(main_kernel, out_shape=(jax.ShapeDtypeStruct((CD, 2 * WD,...  33.3 us
    pallas_call x1, Pallas kernels, exchange_rims(): pl.pallas_call(halo_kernel, out_shape=jax.ShapeDtypeStruct((CD, LEAD + TA...  13 us

profile of v6, /device:TPU:1, one launch (start us, length us, event | category | flops | bytes accessed | tf_op | source)
XLA Modules:
  0.0 48.4 jit_solution(18315738609713029858)
XLA Ops:
  0.6 0.0 copy-start
  0.6 13.0 %rims.1.rims_hbm = bf16[16,1536]{1,0:T(8,128)(2,1)S(1)} custom-call(bf16[16,16000]{1,0:T(8,128)(2,1)} %raw_hbm.1), custom_call_target="tpu_custom_call" | custom-call | tf_op jit(solution)/shard_map/rims/pallas_call | solution.py:71
  13.6 0.0 copy-done
  13.6 33.3 %main.1 = (bf16[16,32,128]{2,1,0:T(8,128)(2,1)S(1)}, f32[2,8,16,512]{3,2,1,0:T(8,128)S(1)}) custom-call(bf16[16,16000]{1,0:T(8,128)(2,1)S(1)} %copy-done, bf16[16,1536]{1,0:T(8,128)(2,1)S(1)} %rims.1.rims_hbm, bf16[2,256,1024]{2,1,0:T(8,128)(2,1)} %constant.4.clone.table_hbm), custom_call_target="tpu_custom_call" | custom-call | tf_op jit(solution)/shard_map/main/pallas_call | solution.py:375
  46.9 0.8 %broadcast_multiply_fusion = f32[2,8,16,512]{3,2,1,0:T(8,128)} fusion(f32[2,8,16,512]{3,2,1,0:T(8,128)S(1)} %get-tuple-element.5), kind=kLoop, calls=%fused_computation | loop fusion | flops 131072 | bytes 1048576 | tf_op jit(solution)/shard_map/mul | solution.py:420
  47.8 0.7 %copy.5 = bf16[128,16,32]{0,2,1:T(8,128)(2,1)} copy(bf16[128,16,32]{0,2,1:T(8,128)(2,1)S(1)} %bitcast.1) | data formatting | bytes 262144
Async XLA Ops:
  0.6 13.0 %copy-start = (bf16[16,16000]{1,0:T(8,128)(2,1)S(1)}, bf16[16,16000]{1,0:T(8,128)(2,1)}, u32[]{:S(2)}) copy-start(bf16[16,16000]{1,0:T(8,128)(2,1)} %raw_hbm.1) | copy-start | bytes 1536004
